TPU v7x, 256 devices: a whole 4x4x8 slice. The times are simulated.
256 devices in a mesh: ctx: 64 (over x, z, core), tp: 4 (over y).
Axes of the slice: x: 4, y: 4, z: 8, core: 2. Of those that a mesh axis runs over, the one named last changes fastest.
Arguments:
- query_head_matrix: bfloat16 [8192, 4096], P('ctx', 'tp'), may hold values from -6 to 6
- key_head_matrix: bfloat16 [8192, 1024], P('ctx', 'tp'), may hold values from -6 to 6
- value_head_matrix: bfloat16 [8192, 1024], P('ctx', 'tp'), may hold values from -6 to 6
- ssm_input: bfloat16 [8192, 8192], P('ctx', 'tp'), may hold values from -0.59765625 to 0.59765625
- log_decay: float32 [8192, 128], P('ctx', 'tp'), may hold values from -1 to 0
- state_write: bfloat16 [8192, 128], P('ctx'), may hold values from -1.796875 to 1.796875
- state_read: bfloat16 [8192, 128], P('ctx'), may hold values from -1.796875 to 1.796875
- document_ids: int32 [8192], P('ctx'), may hold values from 0 to 63, never falling along the last dimension, each value on 1 to 256 neighbouring positions
- attention_output_gradient: bfloat16 [8192, 4096], P('ctx', 'tp'), may hold values from -6 to 6
- cot_mixer: bfloat16 [8192, 8192], P('ctx', 'tp'), may hold values from -6 to 6
Outputs:
- attention_out: bfloat16 [8192, 4096], P('ctx', 'tp')
- mixer_out: bfloat16 [8192, 8192], P('ctx', 'tp')
- grad_key: bfloat16 [8192, 1024], P('ctx', 'tp')
- grad_value: bfloat16 [8192, 1024], P('ctx', 'tp')
- grad_input: bfloat16 [8192, 8192], P('ctx', 'tp')
Inputs may be any that keep to these rules, and one draw needn't show every extreme that they name: `document_ids`: never falls along the sequence; each document holds 1 to 256 tokens.
All inputs are finite; a program needn't handle non-finite values.
Results may differ from a plain program's by a relative error of at most 0.0062.
Values may be sent and summed in bfloat16 or wider, within the bound.
A program may use at most 320 MiB of HBM per device.

v0:
```python
import math

import jax
import jax.numpy as jnp
from jax import lax
from jax.sharding import PartitionSpec as P

HEAD_CHANNELS = 128
SPAN = 2


def passed_along(block, axis, distance):
    devices = range(lax.axis_size(axis))
    route = [(i - distance, i) for i in devices if i - distance in devices]
    return lax.ppermute(block, axis, route)


def prefix(part, axis, combine, identity, reverse):
    count = lax.axis_size(axis)
    place = lax.axis_index(axis)
    ahead = count - 1 - place if reverse else place
    gathered = jax.tree.map(lambda a: lax.all_gather(a, axis), part)
    state = jax.tree.map(lambda a, e: jnp.zeros_like(a) + jnp.asarray(e, a.dtype), part, identity)

    def one(lap, state):
        source = count - 1 - lap if reverse else lap
        return combine(
            state, jax.tree.map(lambda a: lax.dynamic_index_in_dim(a, source, 0, False), gathered)
        )

    return lax.fori_loop(0, ahead, one, state)


def combine_carry(earlier, nearer):
    return (earlier[0] * nearer[0], nearer[0][:, None, None] * earlier[1] + nearer[1])


def mixer_pieces(decays, scores, reads_f32, writes_f32, inside, doc_float, prev_doc):
    running = jnp.cumsum(decays, axis=0).T
    log_gaps = running[:, :, None] - running[:, None, :]
    decay_mat = jnp.exp(jnp.where(inside[None], log_gaps, -jnp.inf))
    weights = (decay_mat * scores[None]).astype(jnp.bfloat16)
    entry_w = jnp.exp(running) * (doc_float == prev_doc).astype(jnp.float32)[None]
    read_w = (entry_w[:, :, None] * reads_f32[None]).astype(jnp.bfloat16)
    exit_w = (
        jnp.exp(running[:, -1:] - running) * (doc_float == doc_float[-1]).astype(jnp.float32)[None]
    )
    write_w = (exit_w[:, :, None] * writes_f32[None]).astype(jnp.bfloat16)
    block_gain = jnp.exp(running[:, -1]) * (doc_float[-1] == prev_doc).astype(jnp.float32)
    weights, read_w, write_w = lax.optimization_barrier((weights, read_w, write_w))
    return (weights, read_w, write_w, block_gain)


def attn_probs(query_grp, key_grp, inside, inv_root):
    scores = (
        jnp.einsum("tid,sd->its", query_grp, key_grp, preferred_element_type=jnp.float32) * inv_root
    )
    scores = jnp.where(inside[None], scores, -jnp.inf)
    row_peak = jnp.max(scores, axis=-1, keepdims=True)
    raised = jnp.exp(scores - row_peak)
    return (raised / jnp.sum(raised, axis=-1, keepdims=True)).astype(jnp.bfloat16)


def attn_grads(query_grp, value_grp, cot_grp, prob_mat, inv_root):
    prob_grad = jnp.einsum("tid,sd->its", cot_grp, value_grp, preferred_element_type=jnp.float32)
    probability_single = prob_mat.astype(jnp.float32)
    inner_sum = jnp.sum(probability_single * prob_grad, axis=-1, keepdims=True)
    score_gradient = (probability_single * (prob_grad - inner_sum) * inv_root).astype(jnp.bfloat16)
    key_gradient = jnp.einsum(
        "its,tid->sd", score_gradient, query_grp, preferred_element_type=jnp.float32
    )
    value_gradient = jnp.einsum(
        "its,tid->sd", prob_mat, cot_grp, preferred_element_type=jnp.float32
    )
    return (key_gradient, value_gradient)


def shards(
    query_head_matrix,
    key_head_matrix,
    value_head_matrix,
    ssm_input,
    log_decay,
    state_write,
    state_read,
    document_ids,
    attention_output_gradient,
    cot_mixer,
):
    tokens = key_head_matrix.shape[0]
    kv_local = key_head_matrix.shape[1] // HEAD_CHANNELS
    queries_per_group = query_head_matrix.shape[1] // (HEAD_CHANNELS * kv_local)
    inv_root = 1.0 / math.sqrt(HEAD_CHANNELS)
    position = lax.axis_index("ctx")
    doc_float = document_ids.astype(jnp.float32)
    doc_wire = document_ids.astype(jnp.bfloat16)
    row_ids = jnp.arange(tokens)

    def assemble(tile_list):
        keys_all = jnp.concatenate(
            [tile_list[num][0] for num in reversed(range(SPAN))] + [key_head_matrix], axis=0
        )
        values_all = jnp.concatenate(
            [tile_list[num][1] for num in reversed(range(SPAN))] + [value_head_matrix], axis=0
        )
        docs_all = jnp.concatenate(
            [tile_list[num][2] for num in reversed(range(SPAN))] + [doc_float], axis=0
        )
        column = jnp.arange(keys_all.shape[0]) - SPAN * tokens
        inside = (docs_all[None, :] == doc_float[:, None]) & (column[None, :] <= row_ids[:, None])
        return (keys_all, values_all, inside)

    first_tiles = []
    for offset in range(1, SPAN + 1):
        fetched = passed_along((key_head_matrix, value_head_matrix, doc_wire), "ctx", offset)
        usable = position >= offset
        first_tiles.append(
            (fetched[0], fetched[1], jnp.where(usable, fetched[2].astype(jnp.float32), -1.0))
        )
    keys_all, values_all, inside_attn = assemble(first_tiles)
    prev_doc = first_tiles[0][2][-1]
    query_grps = []
    cot_grps = []
    fwd_probs = []
    out_cols = []
    for head_grp in range(kv_local):
        low_col = head_grp * queries_per_group * HEAD_CHANNELS
        high_col = (head_grp + 1) * queries_per_group * HEAD_CHANNELS
        query_grp = query_head_matrix[:, low_col:high_col].reshape(
            tokens, queries_per_group, HEAD_CHANNELS
        )
        cot_grp = attention_output_gradient[:, low_col:high_col].reshape(
            tokens, queries_per_group, HEAD_CHANNELS
        )
        prob_mat = attn_probs(
            query_grp,
            keys_all[:, head_grp * HEAD_CHANNELS : (head_grp + 1) * HEAD_CHANNELS],
            inside_attn,
            inv_root,
        )
        out_grp = jnp.einsum(
            "its,sd->tid",
            prob_mat,
            values_all[:, head_grp * HEAD_CHANNELS : (head_grp + 1) * HEAD_CHANNELS],
            preferred_element_type=jnp.float32,
        ).astype(jnp.bfloat16)
        out_cols.append(out_grp.reshape(tokens, queries_per_group * HEAD_CHANNELS))
        query_grps.append(query_grp)
        cot_grps.append(cot_grp)
        fwd_probs.append(prob_mat)
    attention_out = jnp.concatenate(out_cols, axis=1)
    nheads = log_decay.shape[1]
    head_width = ssm_input.shape[1] // nheads
    head_block = math.gcd(nheads, 8)
    block_count = nheads // head_block
    scores_mix = jnp.dot(state_read, state_write.T, preferred_element_type=jnp.float32)
    reads_f32 = state_read.astype(jnp.float32)
    writes_f32 = state_write.astype(jnp.float32)
    inside_mix = (row_ids[:, None] >= row_ids[None, :]) & (doc_float[:, None] == doc_float[None, :])
    block_parts = []
    gain_list = []
    state_list = []
    back_list = []
    for block_no in range(block_count):
        low_col = block_no * head_block * head_width
        high_col = (block_no + 1) * head_block * head_width
        inputs = ssm_input[:, low_col:high_col].reshape(tokens, head_block, head_width)
        cot_rows = cot_mixer[:, low_col:high_col].reshape(tokens, head_block, head_width)
        decays = log_decay[:, block_no * head_block : (block_no + 1) * head_block]
        weights, read_w, write_w, block_gain = mixer_pieces(
            decays, scores_mix, reads_f32, writes_f32, inside_mix, doc_float, prev_doc
        )
        state_list.append(
            jnp.einsum("shp,hsn->hpn", inputs, write_w, preferred_element_type=jnp.float32)
        )
        back_list.append(
            jnp.einsum("thp,htn->hpn", cot_rows, read_w, preferred_element_type=jnp.float32)
        )
        gain_list.append(block_gain)
        block_parts.append((inputs, cot_rows, weights, read_w, write_w))
    block_gains = jnp.concatenate(gain_list, axis=0)
    block_states = jnp.concatenate(state_list, axis=0)
    block_backs = jnp.concatenate(back_list, axis=0)
    identity = (jnp.ones_like(block_gains), jnp.zeros_like(block_states))
    carry_in = prefix((block_gains, block_states), "ctx", combine_carry, identity, False)[1]
    carry_out = prefix((block_gains, block_backs), "ctx", combine_carry, identity, True)[1]
    mixed_cols = []
    grad_cols = []
    for block_no in range(block_count):
        inputs, cot_rows, weights, read_w, write_w = block_parts[block_no]
        low_head = block_no * head_block
        high_head = (block_no + 1) * head_block
        mixed_out = jnp.einsum("hts,shp->thp", weights, inputs, preferred_element_type=jnp.float32)
        mixed_out = mixed_out + jnp.einsum(
            "hpn,htn->thp",
            carry_in[low_head:high_head],
            read_w.astype(jnp.float32),
            precision=lax.Precision.HIGHEST,
        )
        grad_rows = jnp.einsum(
            "hts,thp->shp", weights, cot_rows, preferred_element_type=jnp.float32
        )
        grad_rows = grad_rows + jnp.einsum(
            "hpn,hsn->shp",
            carry_out[low_head:high_head],
            write_w.astype(jnp.float32),
            precision=lax.Precision.HIGHEST,
        )
        mixed_cols.append(mixed_out.astype(jnp.bfloat16).reshape(tokens, head_block * head_width))
        grad_cols.append(grad_rows.astype(jnp.bfloat16).reshape(tokens, head_block * head_width))
    mixer_out = jnp.concatenate(mixed_cols, axis=1)
    grad_input = jnp.concatenate(grad_cols, axis=1)
    second_tiles = []
    for offset in range(1, SPAN + 1):
        fetched = passed_along((key_head_matrix, value_head_matrix, doc_wire), "ctx", offset)
        usable = position >= offset
        second_tiles.append(
            (fetched[0], fetched[1], jnp.where(usable, fetched[2].astype(jnp.float32), -1.0))
        )
    keys_back, values_back, inside_back = assemble(second_tiles)
    saved_probs = [
        attn_probs(
            query_grps[head_grp],
            keys_back[:, head_grp * HEAD_CHANNELS : (head_grp + 1) * HEAD_CHANNELS],
            inside_back,
            inv_root,
        )
        for head_grp in range(kv_local)
    ]
    key_cols = []
    value_cols = []
    for head_grp in range(kv_local):
        key_gradient, value_gradient = attn_grads(
            query_grps[head_grp],
            values_back[:, head_grp * HEAD_CHANNELS : (head_grp + 1) * HEAD_CHANNELS],
            cot_grps[head_grp],
            saved_probs[head_grp],
            inv_root,
        )
        key_cols.append(key_gradient)
        value_cols.append(value_gradient)
    key_window = jnp.concatenate(key_cols, axis=1)
    value_window = jnp.concatenate(value_cols, axis=1)
    key_total = key_window[SPAN * tokens :]
    value_total = value_window[SPAN * tokens :]
    for offset in range(1, SPAN + 1):
        low_row = (SPAN - offset) * tokens
        returned = passed_along(
            (key_window[low_row : low_row + tokens], value_window[low_row : low_row + tokens]),
            "ctx",
            -offset,
        )
        key_total = key_total + returned[0]
        value_total = value_total + returned[1]
    grad_key = key_total.astype(jnp.bfloat16)
    grad_value = value_total.astype(jnp.bfloat16)
    return (attention_out, mixer_out, grad_key, grad_value, grad_input)


def solution(mesh):
    return jax.shard_map(
        shards,
        mesh=mesh,
        in_specs=(
            P("ctx", "tp"),
            P("ctx", "tp"),
            P("ctx", "tp"),
            P("ctx", "tp"),
            P("ctx", "tp"),
            P("ctx", None),
            P("ctx", None),
            P("ctx"),
            P("ctx", "tp"),
            P("ctx", "tp"),
        ),
        out_specs=(P("ctx", "tp"), P("ctx", "tp"), P("ctx", "tp"), P("ctx", "tp"), P("ctx", "tp")),
        check_vma=False,
    )
```

profile of v0, /device:TPU:231, one launch (start us, length us, event | category | flops | bytes accessed | tf_op | source)
XLA Modules:
  0.0 663.1 jit_solution(13718060614326554825)
XLA Ops:
  20.3 1.9 compare_convert_fusion
  22.3 2.1 multiply_convert_fusion.9
  27.3 1.9 fusion.73
  32.3 1.7 copy.257
  44.9 1.7 fusion.75
  48.2 1.7 fusion.74
  51.6 1.7 copy.297
  63.8 1.9 fusion.84
  65.9 138.7 %all-reduce = f32[2048]{0:T(1024)S(1)} all-reduce(f32[2048]{0:T(1024)S(1)} %maximum_dynamic-update-slice_fusion), channel_id=2, replica_groups=mesh['ctx'=64,'tp'=4] {'ctx'}, use_global_device_ids=true, to_apply=%add | all-reduce | flops 2048 | bytes 16384
  207.8 2.2 fusion.79
  212.4 2.2 fusion.78
  217.7 2.0 collective-permute-start.8
  219.8 1.9 collective-permute-start.9
  223.3 2.2 convolution_bitcast_fusion.1
  225.5 2.5 fusion.31
  227.9 2.3 convolution_bitcast_fusion
  230.2 2.5 fusion.30
  232.7 1.8 convolution_convert_fusion.1
  237.9 2.0 collective-permute-start.7
  243.5 1.8 collective-permute-done.7
  247.0 27.9 %all-gather.8.cloned.1.call-done = f32[2048,64,128]{2,1,0:T(8,128)} async-done(((f32[32,64,128]{2,1,0:T(8,128)}), f32[2048,64,128]{2,1,0:T(8,128)}) %all-gather.8.cloned.1.call-update) | async-done | bytes 67108880 | tf_op jit(solution)/shard_map/all_gather | solution.py:22
  283.4 227.2 %all-gather.6.cloned.1.call-done = f32[2048,64,128]{2,1,0:T(8,128)} async-done(((f32[32,64,128]{2,1,0:T(8,128)}), f32[2048,64,128]{2,1,0:T(8,128)}) %all-gather.6.cloned.1.call-update) | async-done | bytes 67108880 | tf_op jit(solution)/shard_map/all_gather | solution.py:22
  510.7 136.1 %while.26 = (s32[]{:T(128)}, f32[32,64,128]{2,1,0:T(8,128)S(1)}, s32[]{:T(128)}, f32[64,32]{1,0:T(8,128)}, f32[64,32,64,128]{3,2,1,0:T(8,128)}, /*index=5*/s32[]{:T(128)}, s32[]{:T(128)}, s32[]{:T(128)}) while((s32[]{:T(128)}, f32[32,64,128]{2,1,0:T(8,128)S(1)}, s32[]{:T(128)}, f32[64,32]{1,0:T(8,128)}, f32[64,32,64,128]{3,2,1,0:T(8,128)}, ...), condition=%wide.region_9.10_spmd, body=%wide.region_8.9_spmd.sunk | while | flops 524293 | bytes 3146239 | solution.py:31
  653.6 1.8 pad_maximum_fusion.3
  (270 shorter events, 211.2 us)
Async XLA Ops:
  7.2 267.7 %all-gather.8.cloned.1.call-start = ((), (), s32[]{:S(2)}) async-start(), calls=%async_computation.1 | async-start | bytes 68157440 | tf_op jit(solution)/shard_map/all_gather | solution.py:22
  7.9 14.3 %copy-start.9 = (bf16[128]{0:T(256)(128)(2,1)}, bf16[128]{0:T(256)(128)(2,1)S(1)}, u32[]{:S(2)}) copy-start(bf16[128]{0:T(256)(128)(2,1)S(1)} %get-tuple-element.252) | copy-start | bytes 772
  7.9 11.6 %collective-permute-start.3 = (bf16[128]{0:T(256)(128)(2,1)S(1)}, bf16[128]{0:T(256)(128)(2,1)S(1)}, u32[]{:S(2)}, u32[]{:S(2)}) collective-permute-start(bf16[128]{0:T(256)(128)(2,1)S(1)} %get-tuple-element.252), channel_id=1, source_target_pairs={{0,4},{4,8},{8,12},{12,16},{16,20},{20,24},{24,28},{28,32},{32,36}... | collective-permute-start | bytes 776 | tf_op jit(solution)/shard_map/ppermute | solution.py:15
  16.0 37.3 %copy-start.6 = (f32[8]{0:T(128)}, f32[8]{0:T(128)S(1)}, u32[]{:S(2)}) copy-start(f32[8]{0:T(128)S(1)} %slice_reduce_fusion.2) | copy-start | bytes 100
  16.5 5.8 copy-start.7
  18.5 11.7 %copy-start.4 = (bf16[128,512]{0,1:T(8,128)(2,1)}, bf16[128,512]{0,1:T(8,128)(2,1)S(1)}, u32[]{:S(2)}) copy-start(bf16[128,512]{0,1:T(8,128)(2,1)S(1)} %copy.273) | copy-start | bytes 393220
  19.3 190.7 %copy-start = (bf16[8,128,128]{2,1,0:T(8,128)(2,1)}, bf16[8,128,128]{2,1,0:T(8,128)(2,1)S(1)}, u32[]{:S(2)}) copy-start(bf16[8,128,128]{2,1,0:T(8,128)(2,1)S(1)} %get-tuple-element.154) | copy-start | bytes 786436
  19.3 190.7 %copy-start.1 = (bf16[8,128,128]{2,1,0:T(8,128)(2,1)}, bf16[8,128,128]{2,1,0:T(8,128)(2,1)S(1)}, u32[]{:S(2)}) copy-start(bf16[8,128,128]{2,1,0:T(8,128)(2,1)S(1)} %get-tuple-element.152) | copy-start | bytes 786436
  19.3 195.3 %copy-start.2 = (bf16[8,128,128]{2,1,0:T(8,128)(2,1)}, bf16[8,128,128]{2,1,0:T(8,128)(2,1)S(1)}, u32[]{:S(2)}) copy-start(bf16[8,128,128]{2,1,0:T(8,128)(2,1)S(1)} %get-tuple-element.145) | copy-start | bytes 786436
  19.4 11.8 %copy-start.5 = (bf16[128,512]{0,1:T(8,128)(2,1)}, bf16[128,512]{0,1:T(8,128)(2,1)S(1)}, u32[]{:S(2)}) copy-start(bf16[128,512]{0,1:T(8,128)(2,1)S(1)} %copy.274) | copy-start | bytes 393220
  19.6 9.6 %copy-start.3 = (bf16[128,512]{0,1:T(8,128)(2,1)}, bf16[128,512]{0,1:T(8,128)(2,1)S(1)}, u32[]{:S(2)}) copy-start(bf16[128,512]{0,1:T(8,128)(2,1)S(1)} %copy.275) | copy-start | bytes 393220
  19.6 0.7 copy-start.8
  27.2 483.4 %all-gather.6.cloned.1.call-start = ((), (), s32[]{:S(2)}) async-start(), calls=%async_computation | async-start | bytes 68157440 | tf_op jit(solution)/shard_map/all_gather | solution.py:22
  36.8 21.3 %collective-permute-start.2 = (bf16[128]{0:T(256)(128)(2,1)}, bf16[128]{0:T(256)(128)(2,1)}, u32[]{:S(2)}, u32[]{:S(2)}) collective-permute-start(bf16[128]{0:T(256)(128)(2,1)} %copy-done.9), channel_id=1, source_target_pairs={{0,8},{4,12},{8,16},{12,20},{16,24},{20,28},{24,32},{28,36},{32,40... | collective-permute-start | bytes 776 | tf_op jit(solution)/shard_map/ppermute | solution.py:15
  38.1 167.2 %collective-permute-start.4 = (bf16[128,256]{1,0:T(8,128)(2,1)}, bf16[128,256]{1,0:T(8,128)(2,1)}, u32[]{:S(2)}, u32[]{:S(2)}) collective-permute-start(bf16[128,256]{1,0:T(8,128)(2,1)} %param.15), channel_id=1, source_target_pairs={{0,8},{4,12},{8,16},{12,20},{16,24},{20,28},{24,32},{28,36},{32,40... | collective-permute-start | bytes 196616 | tf_op jit(solution)/shard_map/ppermute | solution.py:15
  39.4 166.7 %collective-permute-start.5 = (bf16[128,256]{1,0:T(8,128)(2,1)}, bf16[128,256]{1,0:T(8,128)(2,1)}, u32[]{:S(2)}, u32[]{:S(2)}) collective-permute-start(bf16[128,256]{1,0:T(8,128)(2,1)} %param.15), channel_id=1, source_target_pairs={{0,4},{4,8},{8,12},{12,16},{16,20},{20,24},{24,28},{28,32},{32,36}... | collective-permute-start | bytes 196616 | tf_op jit(solution)/shard_map/ppermute | solution.py:15
  42.3 179.4 %collective-permute-start = (bf16[128,256]{0,1:T(8,128)(2,1)}, bf16[128,256]{0,1:T(8,128)(2,1)}, u32[]{:S(2)}, u32[]{:S(2)}) collective-permute-start(bf16[128,256]{0,1:T(8,128)(2,1)} %copy.235), channel_id=1, source_target_pairs={{0,8},{4,12},{8,16},{12,20},{16,24},{20,28},{24,32},{28,36},{32,40... | collective-permute-start | bytes 196616 | tf_op jit(solution)/shard_map/ppermute | solution.py:15
  43.6 178.1 %collective-permute-start.1 = (bf16[128,256]{0,1:T(8,128)(2,1)}, bf16[128,256]{0,1:T(8,128)(2,1)}, u32[]{:S(2)}, u32[]{:S(2)}) collective-permute-start(bf16[128,256]{0,1:T(8,128)(2,1)} %copy.235), channel_id=1, source_target_pairs={{0,4},{4,8},{8,12},{12,16},{16,20},{20,24},{24,28},{28,32},{32,36}... | collective-permute-start | bytes 196616 | tf_op jit(solution)/shard_map/ppermute | solution.py:15
  217.7 24.0 %collective-permute-start.8 = (f32[128,256]{0,1:T(8,128)}, f32[128,256]{0,1:T(8,128)}, u32[]{:S(2)}, u32[]{:S(2)}) collective-permute-start(f32[128,256]{0,1:T(8,128)} %get-tuple-element.212), channel_id=1, source_target_pairs={{4,0},{8,4},{12,8},{16,12},{20,16},{24,20},{28,24},{32,28},{36,32}... | collective-permute-start | bytes 393224 | tf_op jit(solution)/shard_map/ppermute | solution.py:15
  219.8 21.9 %collective-permute-start.9 = (f32[128,256]{0,1:T(8,128)}, f32[128,256]{0,1:T(8,128)}, u32[]{:S(2)}, u32[]{:S(2)}) collective-permute-start(f32[128,256]{0,1:T(8,128)} %get-tuple-element.213), channel_id=1, source_target_pairs={{8,0},{12,4},{16,8},{20,12},{24,16},{28,20},{32,24},{36,28},{40,32... | collective-permute-start | bytes 393224 | tf_op jit(solution)/shard_map/ppermute | solution.py:15
  236.6 6.9 %collective-permute-start.6 = (f32[128,256]{0,1:T(8,128)S(1)}, f32[128,256]{0,1:T(8,128)S(1)}, u32[]{:S(2)}, u32[]{:S(2)}) collective-permute-start(f32[128,256]{0,1:T(8,128)S(1)} %get-tuple-element.214), channel_id=1, source_target_pairs={{4,0},{8,4},{12,8},{16,12},{20,16},{24,20},{28,24},{32,28},{36,32}... | collective-permute-start | bytes 393224 | tf_op jit(solution)/shard_map/ppermute | solution.py:15
  237.9 7.4 %collective-permute-start.7 = (f32[128,256]{0,1:T(8,128)S(1)}, f32[128,256]{0,1:T(8,128)}, u32[]{:S(2)}, u32[]{:S(2)}) collective-permute-start(f32[128,256]{0,1:T(8,128)S(1)} %get-tuple-element.215), channel_id=1, source_target_pairs={{8,0},{12,4},{16,8},{20,12},{24,16},{28,20},{32,24},{36,28},{40,32... | collective-permute-start | bytes 393224 | tf_op jit(solution)/shard_map/ppermute | solution.py:15
Sparse Core Ops, SparseCore 0:
  27.3 247.4 all-gather.7
  277.7 232.9 all-gather.5
where the time goes:
time: 670 us; the launch traced here: 663 us
  waiting for transfers between devices  257 us (38%)
  blocking collectives  139 us (21%)
  other arithmetic  116 us (17%)
  local copies, waits for them, and re-layouts  76.1 us (11%)
  matrix products  41.7 us (6%)
  between operations  16.5 us (2%)
  starting transfers between devices  15 us (2%)
    all_gather x2, waiting for transfers between devices, prefix(): gathered = jax.tree.map(lambda a: lax.all_gather(a, axis), part)  255 us
    unnamed x1, blocking collectives  139 us
    add x63, other arithmetic, combine_carry(): nearer[0][:, None, None] * earlier[1] + nearer[1]  90.7 us
    mul x63, local copies, waits for them, and re-layouts, combine_carry(): nearer[0][:, None, None] * earlier[1] + nearer[1]  43.4 us
    ppermute x10, starting transfers between devices, passed_along(): return lax.ppermute(block, axis, route)  15 us
  transfers between devices with their start and end apart: 12, of which 3 were waited for; matrix products, arithmetic and copies ran while one was open for 12% of the time, Pallas kernels for 0%

commit v1 on v0

v1 whole, which is shorter than its diff:
```python
import math

import jax
import jax.numpy as jnp
from jax import lax
from jax.experimental import pallas as pl
from jax.experimental.pallas import tpu as pltpu
from jax.sharding import PartitionSpec as P

HEAD_CHANNELS = 128
CHUNKS = 4
MESH = pl.DeviceIdType.MESH
F32 = jnp.float32
BF16 = jnp.bfloat16


def dot(a, b, contract=((1,), (0,)), precision=None):
    return lax.dot_general(a, b, (contract, ((), ())), precision=precision, preferred_element_type=F32)


def step_kernel(
    q_in, k_in, v_in, x_in, ld_in, sw_in, sr_in, doc_in, do_in, cm_in,
    ao_out, mo_out, gk_out, gv_out, gx_out,
    qb, dob, xc, ldb, srw, srwt, docs, kw, vw, sc, lt, st, mbuf, cz, zbuf, lbuf, gain, gmate,
    local, outb, aob, pt, dst, bias, gs, gr, gown, gkb, gmask, lsem, ssem, rsem,
):
    tokens = qb.shape[0]
    groups = k_in.shape[1] // HEAD_CHANNELS
    per_group = q_in.shape[1] // k_in.shape[1]
    heads = ld_in.shape[1]
    chunk_cols = x_in.shape[1] // CHUNKS
    chunk_heads = heads // CHUNKS
    half = chunk_cols // chunk_heads
    inv_root = 1.0 / math.sqrt(HEAD_CHANNELS)

    count = lax.axis_size("ctx")
    me = lax.axis_index("ctx")
    row = lax.axis_index("tp")
    side = lax.rem(me, 2)
    other = 1 - side
    after1 = lax.rem(me + 1, count)
    after2 = lax.rem(me + 2, count)
    before1 = lax.rem(me + count - 1, count)
    before2 = lax.rem(me + count - 2, count)
    mate = me + 1 - 2 * side
    outer = lax.rem(me - 1 + 2 * side + count, count)

    local_at = [0]

    def load(src, dst_ref):
        copy = pltpu.make_async_copy(src, dst_ref, lsem.at[local_at[0]])
        local_at[0] += 1
        copy.start()
        return copy

    remote_at = [0]

    def send(src, dst_ref, target):
        n = remote_at[0]
        remote_at[0] += 1
        return pltpu.make_async_remote_copy(
            src_ref=src, dst_ref=dst_ref, send_sem=ssem.at[n], recv_sem=rsem.at[n],
            device_id=(target, row), device_id_type=MESH,
        )

    doc_load = load(doc_in, docs.at[2])
    ld_load = load(ld_in, ldb)
    sw_load = load(sw_in, srw.at[0])
    sr_load = load(sr_in, srw.at[1])
    barrier = pltpu.get_barrier_semaphore()
    for target in (after1, after2, before1, before2):
        pl.semaphore_signal(barrier, inc=1, device_id=(target, row), device_id_type=MESH)
    x_loads = []
    for c in range(CHUNKS):
        cols = pl.ds(c * chunk_cols, chunk_cols)
        x_loads.append((load(x_in.at[:, cols], xc.at[0, c]), load(cm_in.at[:, cols], xc.at[1, c])))
    k_load = load(k_in, kw.at[2])
    v_load = load(v_in, vw.at[2])
    q_load = load(q_in, qb)
    do_load = load(do_in, dob)

    rows_i = lax.broadcasted_iota(jnp.int32, (tokens, tokens), 0)
    cols_i = lax.broadcasted_iota(jnp.int32, (tokens, tokens), 1)
    tril = (rows_i >= cols_i).astype(F32)
    ld_load.wait()
    decays = ldb[...]
    lam = dot(tril, decays, precision=lax.Precision.HIGHEST)
    lam_t = dot(decays, tril, ((0,), (1,)), precision=lax.Precision.HIGHEST)
    for c in range(CHUNKS):
        lt[c] = lam_t[c * chunk_heads : (c + 1) * chunk_heads]
    doc_load.wait()

    doc_row = docs[2].astype(F32)
    doc_rows = jnp.broadcast_to(doc_row, (tokens, tokens))
    doc_cols = doc_rows.T
    doc_last = doc_row[:, tokens - 1 : tokens]

    sw_load.wait()
    sr_load.wait()
    writes = srw[0]
    reads = srw[1]
    srwt[0] = writes.T
    srwt[1] = reads.T

    pl.semaphore_wait(barrier, 4)
    doc_sends = [send(docs.at[2], docs.at[1], after1), send(docs.at[2], docs.at[0], after2)]
    for copy in doc_sends:
        copy.start()
    kv_sends = [
        send(k_in, kw.at[1], after1), send(v_in, vw.at[1], after1),
        send(k_in, kw.at[0], after2), send(v_in, vw.at[0], after2),
    ]
    for copy in kv_sends:
        copy.start()

    spread_at = lax.broadcasted_iota(jnp.int32, (2 * heads, chunk_cols), 0)
    spread_lane = lax.broadcasted_iota(jnp.int32, (2 * heads, chunk_cols), 1)

    def spread(values, slot):
        high = values.astype(BF16)
        low = (values - high.astype(F32)).astype(BF16)
        both = jnp.concatenate([high, low], axis=1)
        for c in range(CHUNKS):
            head = spread_lane // half + c * chunk_heads
            hot = ((spread_at == head) | (spread_at == head + heads)).astype(F32).astype(BF16)
            sc[slot, c] = dot(both, hot)

    lam_last = lam[tokens - 1 : tokens, :]
    doc_cols_h = doc_cols[:, :heads]
    exit_w = jnp.where(doc_cols_h == doc_last, jnp.exp(lam_last - lam), 0.0)
    spread(exit_w, 0)

    same = doc_rows == doc_cols
    score = dot(reads, writes, ((1,), (1,)))
    score_t = dot(writes, reads, ((1,), (1,)))
    gmask[0] = jnp.where(same & (rows_i >= cols_i), score, 0.0)
    gmask[1] = jnp.where(same & (cols_i >= rows_i), score_t, 0.0)

    doc_sends[0].wait_recv()
    doc1_row = jnp.where(me >= 1, docs[1].astype(F32), -1.0)
    prev = doc1_row[:, tokens - 1 : tokens]
    entry_w = jnp.where(doc_cols_h == prev, jnp.exp(lam), 0.0)
    spread(entry_w, 1)
    for c in range(CHUNKS):
        gain[c] = sc[1, c][tokens - 1 : tokens, :]

    for pair in x_loads:
        for copy in pair:
            copy.wait()
    gain_send = send(gain, gmate, mate)
    gain_send.start()

    def state(d, c):
        scaled = (xc[d, c].astype(F32) * sc[d, c]).astype(BF16)
        st[d, c] = dot(srwt[d], scaled).astype(BF16)

    mate_sends = []
    for c in range(CHUNKS):
        state(side, c)
        copy = send(st.at[side, c], mbuf.at[c], mate)
        copy.start()
        mate_sends.append(copy)
    for c in range(CHUNKS):
        state(other, c)
    outer_sends = []
    for c in range(CHUNKS):
        mate_sends[c].wait_recv()
        cz[c] = (st[other, c].astype(F32) + gain[c] * mbuf[c].astype(F32)).astype(BF16)
        copy = send(cz.at[c], zbuf.at[c], outer)
        copy.start()
        outer_sends.append(copy)

    lane = lax.broadcasted_iota(jnp.int32, (1, 2 * half), 1)
    low_half = (lane < half).astype(F32).astype(BF16)
    high_half = (lane >= half).astype(F32).astype(BF16)

    def inside_block(c, carry):
        for j in range(chunk_heads // 2):
            fwd = []
            bwd = []
            for i in range(2):
                h = 2 * j + i
                lam_rows = jnp.broadcast_to(lt[c, h : h + 1, :], (tokens, tokens))
                decay = jnp.exp(-jnp.abs(lam_rows.T - lam_rows))
                fwd.append((decay * gmask[0]).astype(BF16))
                bwd.append((decay * gmask[1]).astype(BF16))
            cols = slice(2 * j * half, (2 * j + 2) * half)
            for d, weights in ((0, fwd), (1, bwd)):
                tile = xc[d, c, :, cols]
                local[d, c, :, cols] = dot(
                    jnp.concatenate(weights, axis=1),
                    jnp.concatenate([tile * low_half, tile * high_half], axis=0),
                )
        return carry

    lax.fori_loop(0, CHUNKS, inside_block, 0)

    doc_sends[1].wait_recv()
    doc2_row = jnp.where(me >= 2, docs[0].astype(F32), -1.0)
    minus = -1e30
    bias[0:tokens] = jnp.where(jnp.broadcast_to(doc2_row, (tokens, tokens)).T == doc_rows, 0.0, minus)
    bias[tokens : 2 * tokens] = jnp.where(
        jnp.broadcast_to(doc1_row, (tokens, tokens)).T == doc_rows, 0.0, minus
    )
    bias[2 * tokens : 3 * tokens] = jnp.where(same & (cols_i >= rows_i), 0.0, minus)
    k_load.wait()
    v_load.wait()
    q_load.wait()
    do_load.wait()
    for copy in kv_sends:
        copy.wait_recv()
    grad_sends = []
    for g in range(groups):
        cols = slice(g * HEAD_CHANNELS, (g + 1) * HEAD_CHANNELS)
        keys = jnp.concatenate([kw[n, :, cols] for n in range(3)], axis=0)
        values = jnp.concatenate([vw[n, :, cols] for n in range(3)], axis=0)
        values_t = values.T
        for i in range(per_group):
            h = g * per_group + i
            hcols = slice(h * HEAD_CHANNELS, (h + 1) * HEAD_CHANNELS)
            icols = slice(i * tokens, (i + 1) * tokens)
            raw = dot(keys, qb[:, hcols], ((1,), (1,))) + bias[...]
            peak = jnp.max(raw, axis=0, keepdims=True)
            raised = jnp.exp((raw - peak) * inv_root)
            probs = (raised * (1.0 / jnp.sum(raised, axis=0, keepdims=True))).astype(BF16)
            pt[:, icols] = probs
            aob[:, hcols] = dot(values_t, probs).T.astype(BF16)
            prob_grad = dot(values, dob[:, hcols], ((1,), (1,)))
            single = probs.astype(F32)
            inner = jnp.sum(single * prob_grad, axis=0, keepdims=True)
            dst[:, icols] = (single * (prob_grad - inner) * inv_root).astype(BF16)
        q_rows = jnp.concatenate(
            [qb[:, h * HEAD_CHANNELS : (h + 1) * HEAD_CHANNELS] for h in range(g * per_group, (g + 1) * per_group)], axis=0
        )
        do_rows = jnp.concatenate(
            [dob[:, h * HEAD_CHANNELS : (h + 1) * HEAD_CHANNELS] for h in range(g * per_group, (g + 1) * per_group)], axis=0
        )
        for n, grad in enumerate((dot(dst[...], q_rows), dot(pt[...], do_rows))):
            gs[g, 0, n] = grad[0:tokens].astype(BF16)
            gs[g, 1, n] = grad[tokens : 2 * tokens].astype(BF16)
            gown[n, :, cols] = grad[2 * tokens :]
        for slot, target in ((1, before1), (0, before2)):
            copy = send(gs.at[g, slot], gr.at[g, slot], target)
            copy.start()
            grad_sends.append(copy)
    ao_store = load(aob, ao_out)

    relay_sends = []
    for c in range(CHUNKS):
        outer_sends[c].wait_recv()
        copy = send(zbuf.at[c], lbuf.at[c], mate)
        copy.start()
        relay_sends.append(copy)

    def finish(d, c, carried):
        outb[d, c] = (local[d, c] + sc[1 - d, c] * dot(srw[1 - d], carried)).astype(BF16)

    for c in range(CHUNKS):
        finish(side, c, zbuf[c])
    gain_send.wait_recv()
    for c in range(CHUNKS):
        relay_sends[c].wait_recv()
        finish(other, c, (mbuf[c].astype(F32) + gmate[c] * lbuf[c].astype(F32)).astype(BF16))
    stores = [ao_store]
    for c in range(CHUNKS):
        cols = pl.ds(c * chunk_cols, chunk_cols)
        stores.append(load(outb.at[0, c], mo_out.at[:, cols]))
        stores.append(load(outb.at[1, c], gx_out.at[:, cols]))

    for copy in grad_sends:
        copy.wait_recv()
    for n in range(2):
        for g in range(groups):
            cols = slice(g * HEAD_CHANNELS, (g + 1) * HEAD_CHANNELS)
            total = gown[n, :, cols] + gr[g, 1, n].astype(F32) + gr[g, 0, n].astype(F32)
            gkb[n, :, cols] = total.astype(BF16)
    stores.append(load(gkb.at[0], gk_out))
    stores.append(load(gkb.at[1], gv_out))

    for copy in doc_sends + kv_sends + [gain_send] + mate_sends + outer_sends + grad_sends + relay_sends:
        copy.wait_send()
    for copy in stores:
        copy.wait()


def shards(q, k, v, x, ld, sw, sr, doc, do, cm):
    tokens = q.shape[0]
    groups = k.shape[1] // HEAD_CHANNELS
    per_group = q.shape[1] // k.shape[1]
    heads = ld.shape[1]
    states = sw.shape[1]
    chunk_cols = x.shape[1] // CHUNKS
    span = 3 * tokens
    remotes = 6 + 1 + 3 * CHUNKS + 2 * groups
    locals_ = 4 + 2 * CHUNKS + 4 + 1 + 2 * CHUNKS + 2
    vmem = pltpu.VMEM
    anywhere = pl.BlockSpec(memory_space=pl.ANY)
    shape = jax.ShapeDtypeStruct
    return pl.pallas_call(
        step_kernel,
        out_shape=(
            shape(q.shape, BF16), shape(x.shape, BF16), shape(k.shape, BF16), shape(v.shape, BF16), shape(x.shape, BF16),
        ),
        in_specs=[anywhere] * 10,
        out_specs=[anywhere] * 5,
        scratch_shapes=[
            vmem(q.shape, BF16),
            vmem(q.shape, BF16),
            vmem((2, CHUNKS, tokens, chunk_cols), BF16),
            vmem(ld.shape, F32),
            vmem((2, tokens, states), BF16),
            vmem((2, states, tokens), BF16),
            vmem((3, 1, tokens), jnp.int32),
            vmem((3,) + k.shape, BF16),
            vmem((3,) + v.shape, BF16),
            vmem((2, CHUNKS, tokens, chunk_cols), F32),
            vmem((CHUNKS, heads // CHUNKS, tokens), F32),
            vmem((2, CHUNKS, states, chunk_cols), BF16),
            vmem((CHUNKS, states, chunk_cols), BF16),
            vmem((CHUNKS, states, chunk_cols), BF16),
            vmem((CHUNKS, states, chunk_cols), BF16),
            vmem((CHUNKS, states, chunk_cols), BF16),
            vmem((CHUNKS, 1, chunk_cols), F32),
            vmem((CHUNKS, 1, chunk_cols), F32),
            vmem((2, CHUNKS, tokens, chunk_cols), F32),
            vmem((2, CHUNKS, tokens, chunk_cols), BF16),
            vmem(q.shape, BF16),
            vmem((span, per_group * tokens), BF16),
            vmem((span, per_group * tokens), BF16),
            vmem((span, tokens), F32),
            vmem((groups, 2, 2, tokens, HEAD_CHANNELS), BF16),
            vmem((groups, 2, 2, tokens, HEAD_CHANNELS), BF16),
            vmem((2,) + k.shape, F32),
            vmem((2,) + k.shape, BF16),
            vmem((2, tokens, tokens), F32),
            pltpu.SemaphoreType.DMA((locals_,)),
            pltpu.SemaphoreType.DMA((remotes,)),
            pltpu.SemaphoreType.DMA((remotes,)),
        ],
        compiler_params=pltpu.CompilerParams(collective_id=0, has_side_effects=True, vmem_limit_bytes=48 << 20),
        name="step",
    )(q, k, v, x, ld, sw, sr, doc.reshape(1, tokens), do, cm)


def solution(mesh):
    both = P("ctx", "tp")
    return jax.shard_map(
        shards,
        mesh=mesh,
        in_specs=(both, both, both, both, both, P("ctx", None), P("ctx", None), P("ctx"), both, both),
        out_specs=(both,) * 5,
        check_vma=False,
    )
```

time: 670 us -> 36.6 us (0.05)
  the two profiles are of different devices: /device:TPU:231 before, /device:TPU:1 now
where the time goes in v1:
time: 36.6 us; the launch traced here: 36.2 us
  Pallas kernels  24.8 us (68%)
  local copies, waits for them, and re-layouts  10.7 us (29%)
  between operations  0.69 us (2%)
    pallas_call x1, Pallas kernels, shards(): pl.pallas_call(step_kernel, out_shape=(shape(q.shape, BF16), shape(x.shap...  24.8 us
    unnamed x24, local copies, waits for them, and re-layouts  10.7 us

profile of v1, /device:TPU:1, one launch (start us, length us, event | category | flops | bytes accessed | tf_op | source)
XLA Modules:
  0.0 36.2 jit_solution(13483765531389937810)
XLA Ops:
  0.6 0.0 copy-start.4
  0.6 0.0 copy-start.8
  0.7 0.8 %copy.15.ld_in = f32[128,32]{1,0:T(8,128)S(1)} copy(f32[128,32]{0,1:T(8,128)} %param.14) | data formatting | bytes 32768 | tf_op args[4]
  1.5 0.0 copy-done.4
  1.5 0.0 copy-done.8
  1.5 0.0 copy-start
  1.5 1.0 %copy-done = bf16[128,2048]{1,0:T(8,128)(2,1)S(1)} copy-done((bf16[128,2048]{1,0:T(8,128)(2,1)S(1)}, bf16[128,2048]{1,0:T(8,128)(2,1)}, u32[]{:S(2)}) %copy-start) | copy-done | bytes 524312
  2.6 0.0 copy-start.1
  2.6 1.0 %copy-done.1 = bf16[128,2048]{1,0:T(8,128)(2,1)S(1)} copy-done((bf16[128,2048]{1,0:T(8,128)(2,1)S(1)}, bf16[128,2048]{1,0:T(8,128)(2,1)}, u32[]{:S(2)}) %copy-start.1) | copy-done | bytes 524312
  3.6 0.0 copy-start.2
  3.6 0.9 %copy-done.2 = bf16[128,1024]{1,0:T(8,128)(2,1)S(1)} copy-done((bf16[128,1024]{1,0:T(8,128)(2,1)S(1)}, bf16[128,1024]{1,0:T(8,128)(2,1)}, u32[]{:S(2)}) %copy-start.2) | copy-done | bytes 262168
  4.6 0.0 copy-start.3
  4.6 0.9 %copy-done.3 = bf16[128,1024]{1,0:T(8,128)(2,1)S(1)} copy-done((bf16[128,1024]{1,0:T(8,128)(2,1)S(1)}, bf16[128,1024]{1,0:T(8,128)(2,1)}, u32[]{:S(2)}) %copy-start.3) | copy-done | bytes 262168
  5.5 0.0 copy-start.5
  5.5 0.8 %copy-done.5 = bf16[128,256]{1,0:T(8,128)(2,1)S(1)} copy-done((bf16[128,256]{1,0:T(8,128)(2,1)S(1)}, bf16[128,256]{1,0:T(8,128)(2,1)}, u32[]{:S(2)}) %copy-start.5) | copy-done | bytes 65560
  6.3 0.0 copy-start.6
  6.3 0.8 %copy-done.6 = bf16[128,128]{1,0:T(8,128)(2,1)S(1)} copy-done((bf16[128,128]{1,0:T(8,128)(2,1)S(1)}, bf16[128,128]{1,0:T(8,128)(2,1)}, u32[]{:S(2)}) %copy-start.6) | copy-done | bytes 32792
  7.1 0.8 %copy-done.7 = bf16[128,128]{1,0:T(8,128)(2,1)S(1)} copy-done((bf16[128,128]{1,0:T(8,128)(2,1)S(1)}, bf16[128,128]{1,0:T(8,128)(2,1)}, u32[]{:S(2)}) %copy-start.7) | copy-done | bytes 32792
  7.9 24.8 %step.1 = (bf16[128,1024]{1,0:T(8,128)(2,1)S(1)}, bf16[128,2048]{1,0:T(8,128)(2,1)S(1)}, bf16[128,256]{1,0:T(8,128)(2,1)S(1)}, bf16[128,256]{1,0:T(8,128)(2,1)S(1)}, bf16[128,2048]{1,0:T(8,128)(2,1)S(1)}) custom-call(bf16[128,1024]{1,0:T(8,128)(2,1)S(1)} %copy-done.2, bf16[128,256]{1,0:T(8,128)(2,1)S(1)} %copy-done.4, bf16[128,256]{1,0:T(8,128)(2,1)S(1)} %copy-done.5, ...), custom_call_target="tpu_custom_call" | custom-call | tf_op jit(solution)/shard_map/step/pallas_call | solution.py:299
  32.6 0.7 %copy.21 = bf16[128,1024]{1,0:T(8,128)(2,1)} copy(bf16[128,1024]{1,0:T(8,128)(2,1)S(1)} %get-tuple-element.10) | data formatting | bytes 524288
  33.3 0.8 %copy.22 = bf16[128,2048]{1,0:T(8,128)(2,1)} copy(bf16[128,2048]{1,0:T(8,128)(2,1)S(1)} %get-tuple-element.11) | data formatting | bytes 1048576
  34.1 0.6 %copy.23 = bf16[128,256]{1,0:T(8,128)(2,1)} copy(bf16[128,256]{1,0:T(8,128)(2,1)S(1)} %get-tuple-element.12) | data formatting | bytes 131072
  34.8 0.6 %copy.24 = bf16[128,256]{1,0:T(8,128)(2,1)} copy(bf16[128,256]{1,0:T(8,128)(2,1)S(1)} %get-tuple-element.13) | data formatting | bytes 131072
  35.4 0.8 %copy.25 = bf16[128,2048]{1,0:T(8,128)(2,1)} copy(bf16[128,2048]{1,0:T(8,128)(2,1)S(1)} %get-tuple-element.14) | data formatting | bytes 1048576
  (1 shorter events, 0.0 us)
Async XLA Ops:
  0.6 0.9 %copy-start.4 = (bf16[128,256]{1,0:T(8,128)(2,1)S(1)}, bf16[128,256]{1,0:T(8,128)(2,1)}, u32[]{:S(2)}) copy-start(bf16[128,256]{1,0:T(8,128)(2,1)} %k_in.1) | copy-start | bytes 196612
  0.6 0.9 %copy-start.8 = (s32[128]{0:T(128)S(1)}, s32[128]{0:T(128)}, u32[]{:S(2)}) copy-start(s32[128]{0:T(128)} %param.17) | copy-start | bytes 1540
  1.5 1.0 %copy-start = (bf16[128,2048]{1,0:T(8,128)(2,1)S(1)}, bf16[128,2048]{1,0:T(8,128)(2,1)}, u32[]{:S(2)}) copy-start(bf16[128,2048]{1,0:T(8,128)(2,1)} %x_in.1) | copy-start | bytes 1572868
  2.6 1.0 %copy-start.1 = (bf16[128,2048]{1,0:T(8,128)(2,1)S(1)}, bf16[128,2048]{1,0:T(8,128)(2,1)}, u32[]{:S(2)}) copy-start(bf16[128,2048]{1,0:T(8,128)(2,1)} %cm_in.1) | copy-start | bytes 1572868
  3.6 0.9 %copy-start.2 = (bf16[128,1024]{1,0:T(8,128)(2,1)S(1)}, bf16[128,1024]{1,0:T(8,128)(2,1)}, u32[]{:S(2)}) copy-start(bf16[128,1024]{1,0:T(8,128)(2,1)} %q_in.1) | copy-start | bytes 786436
  4.6 0.9 %copy-start.3 = (bf16[128,1024]{1,0:T(8,128)(2,1)S(1)}, bf16[128,1024]{1,0:T(8,128)(2,1)}, u32[]{:S(2)}) copy-start(bf16[128,1024]{1,0:T(8,128)(2,1)} %do_in.1) | copy-start | bytes 786436
  5.5 0.8 %copy-start.5 = (bf16[128,256]{1,0:T(8,128)(2,1)S(1)}, bf16[128,256]{1,0:T(8,128)(2,1)}, u32[]{:S(2)}) copy-start(bf16[128,256]{1,0:T(8,128)(2,1)} %v_in.1) | copy-start | bytes 196612
  6.3 0.8 %copy-start.6 = (bf16[128,128]{1,0:T(8,128)(2,1)S(1)}, bf16[128,128]{1,0:T(8,128)(2,1)}, u32[]{:S(2)}) copy-start(bf16[128,128]{1,0:T(8,128)(2,1)} %sw_in.1) | copy-start | bytes 98308
  7.1 0.8 %copy-start.7 = (bf16[128,128]{1,0:T(8,128)(2,1)S(1)}, bf16[128,128]{1,0:T(8,128)(2,1)}, u32[]{:S(2)}) copy-start(bf16[128,128]{1,0:T(8,128)(2,1)} %sr_in.1) | copy-start | bytes 98308

commit v2 on v1

v2 whole, which is shorter than its diff:
```python
import math

import jax
import jax.numpy as jnp
from jax import lax
from jax.experimental import pallas as pl
from jax.experimental.pallas import tpu as pltpu
from jax.sharding import PartitionSpec as P

HEAD_CHANNELS = 128
CHUNKS = 4
MESH = pl.DeviceIdType.MESH
F32 = jnp.float32
BF16 = jnp.bfloat16


def dot(a, b, contract=((1,), (0,)), precision=None):
    return lax.dot_general(a, b, (contract, ((), ())), precision=precision, preferred_element_type=F32)


def step_kernel(
    q_in, k_in, v_in, x_in, ld_in, sw_in, sr_in, doc_in, do_in, cm_in,
    ao, mix, gkv,
    qb, dob, xc, ldb, srw, srwt, docs, kvw, sc, lt, st, mbuf, cz, zbuf, lbuf, gain, gmate,
    local, pt, dst, bias, gs, gr, gown, gmask, lsem, ssem, rsem,
):
    tokens = qb.shape[0]
    groups = k_in.shape[1] // HEAD_CHANNELS
    per_group = q_in.shape[1] // k_in.shape[1]
    heads = ld_in.shape[0]
    chunk_cols = x_in.shape[1] // CHUNKS
    chunk_heads = heads // CHUNKS
    half = chunk_cols // chunk_heads
    inv_root = 1.0 / math.sqrt(HEAD_CHANNELS)
    square = (tokens, tokens)

    count = lax.axis_size("ctx")
    me = lax.axis_index("ctx")
    row = lax.axis_index("tp")
    side = lax.rem(me, 2)
    other = 1 - side
    mate = me + 1 - 2 * side
    outer = me - 1 + 2 * side
    has_before1 = me >= 1
    has_before2 = me >= 2
    has_after1 = me < count - 1
    has_after2 = me < count - 2
    has_outer = has_before1 & has_after1
    is_first = side == 0

    local_at = [0]

    def load(src, dst_ref):
        copy = pltpu.make_async_copy(src, dst_ref, lsem.at[local_at[0]])
        local_at[0] += 1
        copy.start()
        return copy

    remote_at = [0]

    def send(src, dst_ref, target):
        n = remote_at[0]
        remote_at[0] += 1
        return pltpu.make_async_remote_copy(
            src_ref=src, dst_ref=dst_ref, send_sem=ssem.at[n], recv_sem=rsem.at[n],
            device_id=(target, row), device_id_type=MESH,
        )

    docs_mate = send(docs.at[2], docs.at[1 + 2 * side], mate)
    docs_outer = send(docs.at[2], docs.at[3 - 2 * side], outer)
    docs_after2 = send(docs.at[2], docs.at[0], me + 2)
    docs_before2 = send(docs.at[2], docs.at[4], me - 2)
    kv_after1 = [send(kvw.at[2, g], kvw.at[1, g], me + 1) for g in range(groups)]
    kv_after2 = [send(kvw.at[2, g], kvw.at[0, g], me + 2) for g in range(groups)]
    kv_relay = [send(kvw.at[1, g], kvw.at[0, g], mate) for g in range(groups)]
    gain_send = send(gain, gmate, mate)
    mate_sends = [send(st.at[side, c], mbuf.at[c], mate) for c in range(CHUNKS)]
    outer_sends = [send(cz.at[c], zbuf.at[c], outer) for c in range(CHUNKS)]
    relay_sends = [send(zbuf.at[c], lbuf.at[c], mate) for c in range(CHUNKS)]
    grads_before1 = [send(gs.at[g, 1], gr.at[g, 1], me - 1) for g in range(groups)]
    grads_before2 = [send(gs.at[g, 0], gr.at[g, 0], me - 2) for g in range(groups)]

    ld_load = load(ld_in, ldb)
    doc_load = load(doc_in, docs.at[2])
    sw_load = load(sw_in, srw.at[0])
    sr_load = load(sr_in, srw.at[1])
    x_loads = []
    for c in range(CHUNKS):
        cols = pl.ds(c * chunk_cols, chunk_cols)
        x_loads.append((load(x_in.at[:, cols], xc.at[0, c]), load(cm_in.at[:, cols], xc.at[1, c])))
    kv_loads = []
    for g in range(groups):
        cols = pl.ds(g * HEAD_CHANNELS, HEAD_CHANNELS)
        kv_loads.append((load(k_in.at[:, cols], kvw.at[2, g, 0]), load(v_in.at[:, cols], kvw.at[2, g, 1])))
    q_load = load(q_in, qb)
    do_load = load(do_in, dob)

    barrier = pltpu.get_barrier_semaphore()
    for there, target in (
        (has_before1, me - 1), (has_after1, me + 1), (has_before2, me - 2), (has_after2, me + 2)
    ):
        @pl.when(there)
        def _():
            pl.semaphore_signal(barrier, inc=1, device_id=(target, row), device_id_type=MESH)

    @pl.when(jnp.logical_not(has_before1))
    def _():
        docs[1] = jnp.full(docs.shape[1:], -1, jnp.int32)
        kvw[1] = jnp.zeros(kvw.shape[1:], BF16)

    @pl.when(jnp.logical_not(has_before2))
    def _():
        docs[0] = jnp.full(docs.shape[1:], -1, jnp.int32)

        @pl.when(is_first)
        def _():
            kvw[0] = jnp.zeros(kvw.shape[1:], BF16)

    @pl.when(jnp.logical_not(has_after1))
    def _():
        docs[3] = jnp.full(docs.shape[1:], -1, jnp.int32)
        for g in range(groups):
            gr[g, 1] = jnp.zeros(gr.shape[2:], BF16)

    @pl.when(jnp.logical_not(has_after2))
    def _():
        docs[4] = jnp.full(docs.shape[1:], -1, jnp.int32)
        for g in range(groups):
            gr[g, 0] = jnp.zeros(gr.shape[2:], BF16)

    @pl.when(jnp.logical_not(has_outer))
    def _():
        zbuf[...] = jnp.zeros(zbuf.shape, BF16)

    rows_i = lax.broadcasted_iota(jnp.int32, square, 0)
    cols_i = lax.broadcasted_iota(jnp.int32, square, 1)
    triu = (rows_i <= cols_i).astype(F32)
    ld_load.wait()
    lam_t = dot(ldb[...], triu, precision=lax.Precision.HIGHEST)
    for c in range(CHUNKS):
        lt[c] = lam_t[c * chunk_heads : (c + 1) * chunk_heads]

    spread_at = lax.broadcasted_iota(jnp.int32, (2 * heads, chunk_cols), 0)
    spread_lane = lax.broadcasted_iota(jnp.int32, (2 * heads, chunk_cols), 1)

    def spread(values, slot):
        high = values.astype(BF16)
        low = (values - high.astype(F32)).astype(BF16)
        both = jnp.concatenate([high, low], axis=0)
        for c in range(CHUNKS):
            head = spread_lane // half + c * chunk_heads
            hot = ((spread_at == head) | (spread_at == head + heads)).astype(F32).astype(BF16)
            sc[slot, c] = dot(both, hot, ((0,), (0,)))

    spread(jnp.exp(lam_t[:, tokens - 1 : tokens] - lam_t), 0)
    spread(jnp.exp(lam_t), 1)

    doc_load.wait()
    doc_row = docs[2].astype(F32)
    doc_first = doc_row[:, 0:1]
    doc_last = doc_row[:, tokens - 1 : tokens]
    doc_rows = jnp.broadcast_to(doc_row, square)
    doc_cols = doc_rows.T
    same = doc_rows == doc_cols

    sw_load.wait()
    sr_load.wait()
    writes = srw[0]
    reads = srw[1]
    score = dot(reads, writes, ((1,), (1,)))
    score_t = dot(writes, reads, ((1,), (1,)))
    gmask[0] = jnp.where(same & (rows_i >= cols_i), score, 0.0)
    gmask[1] = jnp.where(same & (cols_i >= rows_i), score_t, 0.0)
    writes_in = jnp.where(doc_cols == doc_last, writes.astype(F32), 0.0)
    reads_in = jnp.where(doc_cols == doc_first, reads.astype(F32), 0.0)
    srw[0] = writes_in.astype(BF16)
    srw[1] = reads_in.astype(BF16)
    srwt[0] = writes_in.T.astype(BF16)
    srwt[1] = reads_in.T.astype(BF16)
    whole = (doc_first == doc_last).astype(F32)
    for c in range(CHUNKS):
        gain[c] = sc[1, c, tokens - 1 : tokens, :] * whole

    for pair in x_loads:
        for copy in pair:
            copy.wait()

    def state(d, c):
        scaled = (xc[d, c].astype(F32) * sc[d, c]).astype(BF16)
        st[d, c] = dot(srwt[d], scaled).astype(BF16)

    for c in range(CHUNKS):
        state(side, c)
    for pair in kv_loads:
        for copy in pair:
            copy.wait()

    pl.semaphore_wait(barrier, has_before1.astype(jnp.int32) + has_before2.astype(jnp.int32) + has_after1.astype(jnp.int32) + has_after2.astype(jnp.int32))

    def start(copies, there=None):
        if there is None:
            for copy in copies:
                copy.start()
        else:
            @pl.when(there)
            def _():
                for copy in copies:
                    copy.start()

    def arrived(copies, there=None):
        if there is None:
            for copy in copies:
                copy.wait_recv()
        else:
            @pl.when(there)
            def _():
                for copy in copies:
                    copy.wait_recv()

    def left(copies, there=None):
        if there is None:
            for copy in copies:
                copy.wait_send()
        else:
            @pl.when(there)
            def _():
                for copy in copies:
                    copy.wait_send()

    start([docs_mate])
    start([docs_outer], has_outer)
    start([docs_after2], has_after2)
    start([docs_before2], has_before2)
    start(kv_after1, has_after1)
    start(kv_after2, has_after2 & is_first)
    start([gain_send] + mate_sends)
    for c in range(CHUNKS):
        state(other, c)

    arrived([docs_mate])
    mate_row = docs[3 - 2 * side].astype(F32)
    mate_first = mate_row[:, 0:1]
    mate_last = mate_row[:, tokens - 1 : tokens]
    joined = jnp.where(is_first, mate_first, mate_last) == jnp.where(is_first, doc_last, doc_first)
    joined = joined.astype(F32)
    for c in range(CHUNKS):
        arrived([mate_sends[c]])
        cz[c] = (st[other, c].astype(F32) + (gain[c] * joined) * mbuf[c].astype(F32)).astype(BF16)
        start([outer_sends[c]], has_outer)

    lane = lax.broadcasted_iota(jnp.int32, (1, 2 * half), 1)
    low_half = (lane < half).astype(F32).astype(BF16)
    high_half = (lane >= half).astype(F32).astype(BF16)

    def inside_block(c, carry):
        for j in range(chunk_heads // 2):
            fwd = []
            bwd = []
            for i in range(2):
                h = 2 * j + i
                lam_rows = jnp.broadcast_to(lt[c, h : h + 1, :], square)
                decay = jnp.exp(-jnp.abs(lam_rows.T - lam_rows))
                fwd.append((decay * gmask[0]).astype(BF16))
                bwd.append((decay * gmask[1]).astype(BF16))
            cols = slice(2 * j * half, (2 * j + 2) * half)
            for d, weights in ((0, fwd), (1, bwd)):
                tile = xc[d, c, :, cols]
                local[d, c, :, cols] = dot(
                    jnp.concatenate(weights, axis=1),
                    jnp.concatenate([tile * low_half, tile * high_half], axis=0),
                )
        return carry

    lax.fori_loop(0, CHUNKS, inside_block, 0)

    arrived([docs_outer], has_outer)
    arrived([docs_after2], has_before2)
    arrived([docs_before2], has_after2)
    q_load.wait()
    do_load.wait()
    minus = -1e30
    for n in range(2):
        before = jnp.broadcast_to(docs[n].astype(F32), square).T
        bias[n * tokens : (n + 1) * tokens] = jnp.where(before == doc_rows, 0.0, minus)
    bias[2 * tokens : 3 * tokens] = jnp.where(same & (cols_i >= rows_i), 0.0, minus)
    for g in range(groups):
        arrived([kv_after1[g]], has_before1)
        start([kv_relay[g]], is_first)
        arrived([kv_after2[g]], has_before2 & is_first)
        arrived([kv_relay[g]], side == 1)
        cols = slice(g * HEAD_CHANNELS, (g + 1) * HEAD_CHANNELS)
        keys = jnp.concatenate([kvw[n, g, 0] for n in range(3)], axis=0)
        values = jnp.concatenate([kvw[n, g, 1] for n in range(3)], axis=0)
        values_t = values.T
        group_heads = range(g * per_group, (g + 1) * per_group)
        for i, h in enumerate(group_heads):
            hcols = slice(h * HEAD_CHANNELS, (h + 1) * HEAD_CHANNELS)
            icols = slice(i * tokens, (i + 1) * tokens)
            raw = dot(keys, qb[:, hcols], ((1,), (1,))) + bias[...]
            peak = jnp.max(raw, axis=0, keepdims=True)
            raised = jnp.exp((raw - peak) * inv_root)
            probs = (raised * (1.0 / jnp.sum(raised, axis=0, keepdims=True))).astype(BF16)
            pt[:, icols] = probs
            ao[:, hcols] = dot(values_t, probs).T.astype(BF16)
            prob_grad = dot(values, dob[:, hcols], ((1,), (1,)))
            single = probs.astype(F32)
            inner = jnp.sum(single * prob_grad, axis=0, keepdims=True)
            dst[:, icols] = (single * (prob_grad - inner) * inv_root).astype(BF16)
        q_rows, do_rows = (
            jnp.concatenate([ref[:, h * HEAD_CHANNELS : (h + 1) * HEAD_CHANNELS] for h in group_heads], axis=0)
            for ref in (qb, dob)
        )
        for n, grad in enumerate((dot(dst[...], q_rows), dot(pt[...], do_rows))):
            gs[g, 0, n] = grad[0:tokens].astype(BF16)
            gs[g, 1, n] = grad[tokens : 2 * tokens].astype(BF16)
            gown[n, :, cols] = grad[2 * tokens :]
        start([grads_before1[g]], has_before1)
        start([grads_before2[g]], has_before2)

    for c in range(CHUNKS):
        arrived([outer_sends[c]], has_outer)
        start([relay_sends[c]])

    outer_row = docs[1 + 2 * side].astype(F32)
    far_row = docs[4 - 4 * side].astype(F32)
    outer_joined = jnp.where(is_first, outer_row[:, tokens - 1 : tokens], outer_row[:, 0:1]) == jnp.where(
        is_first, doc_first, doc_last
    )
    mate_joined = jnp.where(is_first, mate_last, mate_first) == jnp.where(
        is_first, far_row[:, 0:1], far_row[:, tokens - 1 : tokens]
    )
    mate_joined = mate_joined.astype(F32)

    def finish(d, c, rows, carried):
        cols = slice(c * chunk_cols, (c + 1) * chunk_cols)
        mix[d, :, cols] = (local[d, c] + sc[1 - d, c] * dot(rows, carried)).astype(BF16)

    rows = (srw[other].astype(F32) * outer_joined.astype(F32)).astype(BF16)
    for c in range(CHUNKS):
        finish(side, c, rows, zbuf[c])
    rows = (srw[side].astype(F32) * joined).astype(BF16)
    arrived([gain_send])
    for c in range(CHUNKS):
        arrived([relay_sends[c]])
        carried = mbuf[c].astype(F32) + (gmate[c] * mate_joined) * lbuf[c].astype(F32)
        finish(other, c, rows, carried.astype(BF16))

    arrived(grads_before1, has_after1)
    arrived(grads_before2, has_after2)
    for n in range(2):
        for g in range(groups):
            cols = slice(g * HEAD_CHANNELS, (g + 1) * HEAD_CHANNELS)
            total = gown[n, :, cols] + gr[g, 1, n].astype(F32) + gr[g, 0, n].astype(F32)
            gkv[n, :, cols] = total.astype(BF16)

    left([docs_mate, gain_send] + mate_sends + relay_sends)
    left([docs_outer] + outer_sends, has_outer)
    left([docs_after2], has_after2)
    left([docs_before2] + grads_before2, has_before2)
    left(kv_after1, has_after1)
    left(kv_after2, has_after2 & is_first)
    left(kv_relay, is_first)
    left(grads_before1, has_before1)


def store_kernel(ao, mix, gkv, ao_out, mo_out, gk_out, gv_out, gx_out, sem):
    copies = [
        pltpu.make_async_copy(src, dst, sem.at[n])
        for n, (src, dst) in enumerate(
            ((mix.at[0], mo_out), (mix.at[1], gx_out), (ao, ao_out), (gkv.at[0], gk_out), (gkv.at[1], gv_out))
        )
    ]
    for copy in copies:
        copy.start()
    for copy in copies:
        copy.wait()


def shards(q, k, v, x, ld, sw, sr, doc, do, cm):
    tokens = q.shape[0]
    groups = k.shape[1] // HEAD_CHANNELS
    per_group = q.shape[1] // k.shape[1]
    heads = ld.shape[1]
    states = sw.shape[1]
    chunk_cols = x.shape[1] // CHUNKS
    span = 3 * tokens
    remotes = 4 + 3 * groups + 1 + 3 * CHUNKS + 2 * groups
    locals_ = 4 + 2 * CHUNKS + 2 * groups + 2
    vmem = pltpu.VMEM
    hbm = pl.BlockSpec(memory_space=pltpu.HBM)
    onchip = pl.BlockSpec(memory_space=pltpu.VMEM)
    shape = jax.ShapeDtypeStruct
    operands = [
        pltpu.with_memory_space_constraint(a, pltpu.HBM) for a in (q, k, v, x, ld.T, sw, sr, doc.reshape(1, tokens), do, cm)
    ]
    parts = pl.pallas_call(
        step_kernel,
        out_shape=(shape(q.shape, BF16), shape((2,) + x.shape, BF16), shape((2,) + k.shape, BF16)),
        in_specs=[hbm] * 10,
        out_specs=[onchip] * 3,
        scratch_shapes=[
            vmem(q.shape, BF16),
            vmem(q.shape, BF16),
            vmem((2, CHUNKS, tokens, chunk_cols), BF16),
            vmem((heads, tokens), F32),
            vmem((2, tokens, states), BF16),
            vmem((2, states, tokens), BF16),
            vmem((5, 1, tokens), jnp.int32),
            vmem((3, groups, 2, tokens, HEAD_CHANNELS), BF16),
            vmem((2, CHUNKS, tokens, chunk_cols), F32),
            vmem((CHUNKS, heads // CHUNKS, tokens), F32),
            vmem((2, CHUNKS, states, chunk_cols), BF16),
            vmem((CHUNKS, states, chunk_cols), BF16),
            vmem((CHUNKS, states, chunk_cols), BF16),
            vmem((CHUNKS, states, chunk_cols), BF16),
            vmem((CHUNKS, states, chunk_cols), BF16),
            vmem((CHUNKS, 1, chunk_cols), F32),
            vmem((CHUNKS, 1, chunk_cols), F32),
            vmem((2, CHUNKS, tokens, chunk_cols), F32),
            vmem((span, per_group * tokens), BF16),
            vmem((span, per_group * tokens), BF16),
            vmem((span, tokens), F32),
            vmem((groups, 2, 2, tokens, HEAD_CHANNELS), BF16),
            vmem((groups, 2, 2, tokens, HEAD_CHANNELS), BF16),
            vmem((2,) + k.shape, F32),
            vmem((2, tokens, tokens), F32),
            pltpu.SemaphoreType.DMA((locals_,)),
            pltpu.SemaphoreType.DMA((remotes,)),
            pltpu.SemaphoreType.DMA((remotes,)),
        ],
        compiler_params=pltpu.CompilerParams(collective_id=0, has_side_effects=True, vmem_limit_bytes=40 << 20),
        name="step",
    )(*operands)
    return pl.pallas_call(
        store_kernel,
        out_shape=(
            shape(q.shape, BF16), shape(x.shape, BF16), shape(k.shape, BF16), shape(v.shape, BF16), shape(x.shape, BF16),
        ),
        in_specs=[onchip] * 3,
        out_specs=[hbm] * 5,
        scratch_shapes=[pltpu.SemaphoreType.DMA((5,))],
        compiler_params=pltpu.CompilerParams(vmem_limit_bytes=8 << 20),
        name="store",
    )(*parts)


def solution(mesh):
    both = P("ctx", "tp")
    return jax.shard_map(
        shards,
        mesh=mesh,
        in_specs=(both, both, both, both, both, P("ctx", None), P("ctx", None), P("ctx"), both, both),
        out_specs=(both,) * 5,
        check_vma=False,
    )
```

time: 36.6 us -> 21.9 us (0.60)
  the two profiles are of different devices: /device:TPU:1 before, /device:TPU:23 now
where the time goes in v2:
time: 21.9 us; the launch traced here: 21.7 us
  Pallas kernels  21.1 us (96%)
  between operations  0.64 us (3%)
    pallas_call x1, Pallas kernels, shards(): pl.pallas_call(step_kernel, out_shape=(shape(q.shape, BF16), shape((2,) +...  19.9 us
    pallas_call x1, Pallas kernels, shards(): pl.pallas_call(store_kernel, out_shape=(shape(q.shape, BF16), shape(x.sha...  1.13 us

profile of v2, /device:TPU:23, one launch (start us, length us, event | category | flops | bytes accessed | tf_op | source)
XLA Modules:
  0.0 21.7 jit_solution(17708404181144832836)
XLA Ops:
  0.6 19.9 %step.1 = (bf16[128,1024]{1,0:T(8,128)(2,1)S(1)}, bf16[2,128,2048]{2,1,0:T(8,128)(2,1)S(1)}, bf16[2,128,256]{2,1,0:T(8,128)(2,1)S(1)}) custom-call(bf16[128,1024]{1,0:T(8,128)(2,1)} %q_in.1, bf16[128,256]{1,0:T(8,128)(2,1)} %k_in.1, bf16[128,256]{1,0:T(8,128)(2,1)} %v_in.1, bf16[128,2048]{1,0:T(8,128)(2,1)} %x_in.1, f32[32,128]{1,0:T(8,128)} %bitcast.2, ...), custom_call_target="tpu_custom_call" | custom-call | tf_op jit(solution)/shard_map/step/pallas_call | solution.py:396
  20.6 1.1 %store.1 = (bf16[128,1024]{1,0:T(8,128)(2,1)}, bf16[128,2048]{1,0:T(8,128)(2,1)}, bf16[128,256]{1,0:T(8,128)(2,1)}, bf16[128,256]{1,0:T(8,128)(2,1)}, bf16[128,2048]{1,0:T(8,128)(2,1)}) custom-call(bf16[128,1024]{1,0:T(8,128)(2,1)S(1)} %get-tuple-element.8.ao, bf16[2,128,2048]{2,1,0:T(8,128)(2,1)S(1)} %get-tuple-element.9.mix, ...), custom_call_target="tpu_custom_call" | custom-call | tf_op jit(solution)/shard_map/store/pallas_call | solution.py:434

commit v3 on v2

v3 whole, which is shorter than its diff:
```python
import math

import jax
import jax.numpy as jnp
from jax import lax
from jax.experimental import pallas as pl
from jax.experimental.pallas import tpu as pltpu
from jax.sharding import PartitionSpec as P

HEAD_CHANNELS = 128
CHUNKS = 4
ROUND = 16
MESH = pl.DeviceIdType.MESH
F32 = jnp.float32
BF16 = jnp.bfloat16


def dot(a, b, contract=((1,), (0,))):
    return lax.dot_general(a, b, (contract, ((), ())), preferred_element_type=F32)


def bf16_parts(values, count):
    parts = []
    for _ in range(count):
        parts.append(values.astype(BF16))
        values = values - parts[-1].astype(F32)
    return jnp.concatenate(parts, axis=0)


def step_kernel(
    q_in, k_in, v_in, x_in, ld_in, sw_in, sr_in, doc_in, do_in, cm_in,
    ao, mix, gkv,
    qw, dow, xc, ldb, srw, srwt, docs, kvo, kvw, scale, wrow, sc, lt, st, mbuf, cz, zbuf, lbuf, gain, gmate,
    local, pt, dst, bias, aob, aom, gs, gacc, gr, gsm, grm, gmask, lsem, ssem, rsem,
):
    tokens = qw.shape[1]
    wide = qw.shape[2]
    heads = ld_in.shape[0]
    per_group = wide // HEAD_CHANNELS
    chunk_cols = x_in.shape[1] // CHUNKS
    chunk_heads = heads // CHUNKS
    half = chunk_cols // chunk_heads
    inv_root = 1.0 / math.sqrt(HEAD_CHANNELS)
    square = (tokens, tokens)

    count = lax.axis_size("ctx")
    me = lax.axis_index("ctx")
    row = lax.axis_index("tp")
    side = lax.rem(me, 2)
    other = 1 - side
    own = 2 + side
    mate = me + 1 - 2 * side
    outer = me - 1 + 2 * side
    before = [me - side - 2, me - side - 1]
    after = [me - side + 2, me - side + 3]
    has_before = me >= 2
    has_after = me < count - 2
    is_first = side == 0
    has_outer = (is_first & has_before) | (jnp.logical_not(is_first) & has_after)

    local_at = [0]

    def load(src, dst_ref):
        copy = pltpu.make_async_copy(src, dst_ref, lsem.at[local_at[0]])
        local_at[0] += 1
        copy.start()
        return copy

    send_at = [0]
    recv_at = [0]

    def slot(at, n=1):
        at[0] += n
        return at[0] - n

    def copy_to(src, dst_ref, target, recv):
        return pltpu.make_async_remote_copy(
            src_ref=src, dst_ref=dst_ref, send_sem=ssem.at[slot(send_at)], recv_sem=rsem.at[recv],
            device_id=(target, row), device_id_type=MESH,
        )

    def send(src, dst_ref, target):
        return copy_to(src, dst_ref, target, slot(recv_at))

    def each(copies, act, there):
        if there is None:
            for copy in copies:
                act(copy)
        else:
            @pl.when(there)
            def _():
                for copy in copies:
                    act(copy)

    def start(copies, there=None):
        each(copies, lambda copy: copy.start(), there)

    def arrived(copies, there=None):
        each(copies, lambda copy: copy.wait_recv(), there)

    def left(copies, there=None):
        each(copies, lambda copy: copy.wait_send(), there)

    def over(count, body):
        lax.fori_loop(0, count, lambda c, carry: (body(c), carry)[1], 0)

    def part(which, width):
        return pl.ds(pl.multiple_of(which * width, width), width)

    docs_mate = send(docs.at[own], docs.at[own], mate)
    at = slot(recv_at, 2)
    docs_after = [copy_to(docs.at[own], docs.at[side], after[h], at + side) for h in range(2)]
    docs_from = [copy_to(docs.at[own], docs.at[h], mate, at + h) for h in range(2)]
    at = slot(recv_at)
    docs_before = [copy_to(docs.at[2], docs.at[4], before[h], at) for h in range(2)]
    kv_mate = send(kvo.at[other], kvw.at[own], mate)
    at = slot(recv_at, 2)
    kv_after = [copy_to(kvo.at[h], kvw.at[side], after[h], at + side) for h in range(2)]
    kv_from = [copy_to(kvo.at[h], kvw.at[h], mate, at + h) for h in range(2)]
    q_mate = send(q_in.at[:, part(other, wide)], qw.at[side], mate)
    do_mate = send(do_in.at[:, part(other, wide)], dow.at[side], mate)
    gain_send = send(gain, gmate, mate)

    def chunked(src, dst_ref, target):
        base_send, base_recv = slot(send_at, CHUNKS), slot(recv_at, CHUNKS)

        def copy(c):
            return pltpu.make_async_remote_copy(
                src_ref=src.at[c], dst_ref=dst_ref.at[c], send_sem=ssem.at[base_send + c], recv_sem=rsem.at[base_recv + c],
                device_id=(target, row), device_id_type=MESH,
            )

        return copy

    mate_send = chunked(st.at[side], mbuf, mate)
    outer_send = chunked(cz, zbuf, outer)
    relay_send = chunked(zbuf, lbuf, mate)
    ao_mate = send(aob.at[other], aom, mate)
    at = slot(recv_at, 2)
    grads_at = slot(send_at, 2)

    def grads_before(h):
        return pltpu.make_async_remote_copy(
            src_ref=gs.at[h], dst_ref=gr.at[side], send_sem=ssem.at[grads_at + h], recv_sem=rsem.at[at + side],
            device_id=(before[0] + h, row), device_id_type=MESH,
        )

    grads_from = [copy_to(gs.at[h], gr.at[h], mate, at + h) for h in range(2)]
    grads_mate = send(gsm, grm, mate)

    barrier = pltpu.get_barrier_semaphore()
    for there, targets in ((None, [mate]), (has_before, before), (has_after, after)):
        each(
            targets,
            lambda target: pl.semaphore_signal(barrier, inc=1, device_id=(target, row), device_id_type=MESH),
            there,
        )

    doc_load = load(doc_in, docs.at[own])
    kv_loads = []
    for h in range(2):
        cols = pl.ds(h * HEAD_CHANNELS, HEAD_CHANNELS)
        kv_loads += [load(k_in.at[:, cols], kvo.at[h, 0]), load(v_in.at[:, cols], kvo.at[h, 1])]
    ld_load = load(ld_in, ldb)
    sw_load = load(sw_in, srw.at[0])
    sr_load = load(sr_in, srw.at[1])
    x_at = local_at[0]
    local_at[0] += 2
    for d, src in enumerate((x_in, cm_in)):
        for c in range(CHUNKS):
            pltpu.make_async_copy(src.at[:, pl.ds(c * chunk_cols, chunk_cols)], xc.at[d, c], lsem.at[x_at + d]).start()
    own_loads = [
        load(k_in.at[:, part(side, HEAD_CHANNELS)], kvw.at[own, 0]),
        load(v_in.at[:, part(side, HEAD_CHANNELS)], kvw.at[own, 1]),
        load(q_in.at[:, part(side, wide)], qw.at[side]),
        load(do_in.at[:, part(side, wide)], dow.at[side]),
    ]

    @pl.when(jnp.logical_not(has_before))
    def _():
        for h in range(2):
            docs[h] = jnp.full(docs.shape[1:], -1, jnp.int32)
            kvw[h] = jnp.zeros(kvw.shape[1:], BF16)

    @pl.when(jnp.logical_not(has_after))
    def _():
        docs[4] = jnp.full(docs.shape[1:], -1, jnp.int32)
        gr[...] = jnp.zeros(gr.shape, BF16)

    @pl.when(jnp.logical_not(has_outer))
    def _():
        zbuf[...] = jnp.zeros(zbuf.shape, BF16)

    def announce():
        pl.semaphore_wait(barrier, 1 + 2 * has_before.astype(jnp.int32) + 2 * has_after.astype(jnp.int32))
        start([docs_mate])
        start(docs_after + kv_after, has_after)
        start(docs_before, has_before & is_first)
        start([kv_mate, q_mate, do_mate])

    sends_early = lax.rem(me, ROUND) >= ROUND // 2
    doc_load.wait()
    for copy in kv_loads:
        copy.wait()

    @pl.when(sends_early)
    def _():
        announce()

    rows_i = lax.broadcasted_iota(jnp.int32, square, 0)
    cols_i = lax.broadcasted_iota(jnp.int32, square, 1)
    triu = (rows_i <= cols_i).astype(F32).astype(BF16)
    ld_load.wait()
    sums = dot(bf16_parts(ldb[...], 3), triu)
    lam_t = (sums[2 * heads :] + sums[heads : 2 * heads]) + sums[:heads]
    for c in range(CHUNKS):
        lt[c] = lam_t[c * chunk_heads : (c + 1) * chunk_heads]
    exits = jnp.exp(lam_t[:, tokens - 1 : tokens] - lam_t)
    entries = jnp.exp(lam_t)
    for c in range(CHUNKS):
        wrow[0, c] = exits[c * chunk_heads : (c + 1) * chunk_heads]
        wrow[1, c] = entries[c * chunk_heads : (c + 1) * chunk_heads]

    doc_row = docs[own].astype(F32)
    doc_first = doc_row[:, 0:1]
    doc_last = doc_row[:, tokens - 1 : tokens]
    doc_rows = jnp.broadcast_to(doc_row, square)
    doc_cols = doc_rows.T
    sw_load.wait()
    sr_load.wait()
    writes = srw[0]
    reads = srw[1]
    writes_in = jnp.where(doc_cols == doc_last, writes.astype(F32), 0.0)
    reads_in = jnp.where(doc_cols == doc_first, reads.astype(F32), 0.0)
    srw[0] = writes_in.astype(BF16)
    srw[1] = reads_in.astype(BF16)
    srwt[0] = writes_in.T
    srwt[1] = reads_in.T

    lane = lax.broadcasted_iota(jnp.int32, (1, 2 * half), 1)
    low_half = (lane < half).astype(F32).astype(BF16)
    high_half = (lane >= half).astype(F32).astype(BF16)

    def two_heads(tile):
        return jnp.concatenate([tile * low_half, tile * high_half], axis=0)

    def state(d, c):
        weights = wrow[d, c]
        for j in range(chunk_heads // 2):
            cols = slice(2 * j * half, (2 * j + 2) * half)
            left_side = [(srwt[d] * weights[h : h + 1]).astype(BF16) for h in (2 * j, 2 * j + 1)]
            st[d, c, :, cols] = dot(jnp.concatenate(left_side, axis=1), two_heads(xc[d, c, :, cols])).astype(BF16)

    for d in range(2):
        pltpu.make_async_copy(xc.at[d], xc.at[d], lsem.at[x_at + d]).wait()

    def first_state(c):
        state(side, c)
        start([mate_send(c)], sends_early)

    over(CHUNKS, first_state)

    @pl.when(jnp.logical_not(sends_early))
    def _():
        announce()
        over(CHUNKS, lambda c: mate_send(c).start())

    over(CHUNKS, lambda c: state(other, c))

    whole = (doc_first == doc_last).astype(F32)

    def gains(c):
        ends = wrow[1, c][:, tokens - 1 : tokens] * whole
        pairs = [
            jnp.where(lane < half, ends[h : h + 1], ends[h + 1 : h + 2]) for h in range(0, chunk_heads, 2)
        ]
        gain[c] = jnp.concatenate(pairs, axis=1)

    over(CHUNKS, gains)
    start([gain_send])

    def edge(early, late):
        ends = docs[early].astype(F32)[:, tokens - 1 : tokens]
        return (docs[late].astype(F32)[:, 0:1] == ends).astype(F32)

    arrived([docs_mate])
    joined = edge(2, 3)

    def combine(c):
        mate_send(c).wait_recv()
        cz[c] = (st[other, c].astype(F32) + (gain[c] * joined) * mbuf[c].astype(F32)).astype(BF16)
        start([outer_send(c)], has_outer)

    over(CHUNKS, combine)

    scale[0] = bf16_parts(exits, 2).T
    scale[1] = bf16_parts(entries, 2).T
    spread_at = lax.broadcasted_iota(jnp.int32, (2 * heads, chunk_cols), 0)
    spread_head = lax.broadcasted_iota(jnp.int32, (2 * heads, chunk_cols), 1) // half

    same = doc_rows == doc_cols
    gmask[0] = jnp.where(same & (rows_i >= cols_i), dot(reads, writes, ((1,), (1,))), 0.0)
    gmask[1] = jnp.where(same & (cols_i >= rows_i), dot(writes, reads, ((1,), (1,))), 0.0)

    def inside_block(c):
        head = spread_head + c * chunk_heads
        hot = ((spread_at == head) | (spread_at == head + heads)).astype(F32).astype(BF16)
        for d in range(2):
            sc[d, c] = dot(scale[d], hot)
        for j in range(chunk_heads // 2):
            fwd = []
            bwd = []
            for h in (2 * j, 2 * j + 1):
                lam_rows = jnp.broadcast_to(lt[c, h : h + 1, :], square)
                decay = jnp.exp(-jnp.abs(lam_rows.T - lam_rows))
                fwd.append((decay * gmask[0]).astype(BF16))
                bwd.append((decay * gmask[1]).astype(BF16))
            cols = slice(2 * j * half, (2 * j + 2) * half)
            for d, weights in ((0, fwd), (1, bwd)):
                local[d, c, :, cols] = dot(jnp.concatenate(weights, axis=1), two_heads(xc[d, c, :, cols]))

    over(CHUNKS, inside_block)

    arrived(docs_from, has_before)
    for copy in own_loads:
        copy.wait()
    arrived([q_mate, do_mate, kv_mate])
    arrived(kv_from, has_before)
    gacc[...] = jnp.zeros(gacc.shape, F32)

    def attend(pos):
        rows = jnp.broadcast_to(docs[2 + pos].astype(F32), square)
        for n in range(3):
            keep = jnp.broadcast_to(docs[pos + n].astype(F32), square).T == rows
            if n == 2:
                keep = keep & (cols_i >= rows_i)
            bias[n * tokens : (n + 1) * tokens] = jnp.where(keep, 0.0, -1e30)

        def two_queries(pair):
            def pair_of(ref):
                return jnp.concatenate(
                    [ref[pos, :, pl.ds(pl.multiple_of((2 * pair + i) * HEAD_CHANNELS, HEAD_CHANNELS), HEAD_CHANNELS)] for i in range(2)],
                    axis=0,
                )

            keys = jnp.concatenate([kvw[pos + n, 0] for n in range(3)], axis=0)
            values = jnp.concatenate([kvw[pos + n, 1] for n in range(3)], axis=0)
            mask = jnp.concatenate([bias[...], bias[...]], axis=1)
            raw = dot(keys, pair_of(qw), ((1,), (1,))) + mask
            peak = jnp.max(raw, axis=0, keepdims=True)
            raised = jnp.exp((raw - peak) * inv_root)
            probs = (raised * (1.0 / jnp.sum(raised, axis=0, keepdims=True))).astype(BF16)
            pt[pair] = probs
            out_t = dot(values.T, probs)
            for i in range(2):
                cols = pl.ds(pl.multiple_of((2 * pair + i) * HEAD_CHANNELS, HEAD_CHANNELS), HEAD_CHANNELS)
                aob[pos, :, cols] = out_t[:, i * tokens : (i + 1) * tokens].T.astype(BF16)
            prob_grad = dot(values, pair_of(dow), ((1,), (1,)))
            single = probs.astype(F32)
            inner = jnp.sum(single * prob_grad, axis=0, keepdims=True)
            dst[pair] = (single * (prob_grad - inner) * inv_root).astype(BF16)

        over(per_group // 2, two_queries)
        for n, (probs_ref, rows_ref) in enumerate(((dst, qw), (pt, dow))):
            grad = dot(
                jnp.concatenate([probs_ref[pair] for pair in range(per_group // 2)], axis=1),
                jnp.concatenate(
                    [rows_ref[pos, :, i * HEAD_CHANNELS : (i + 1) * HEAD_CHANNELS] for i in range(per_group)], axis=0
                ),
            )
            for m in range(3):
                gacc[pos + m, n] += grad[m * tokens : (m + 1) * tokens]
            gs[pos, n] = gacc[pos, n].astype(BF16)
        start([grads_before(pos)], has_before)

    over(2, attend)
    start([ao_mate])
    for n in range(2):
        gsm[n] = gacc[2 + other, n].astype(BF16)
    start([grads_mate])
    ao[side] = aob[side]

    arrived([docs_before[0]], has_after)
    in_before = edge(1, 2)
    in_after = edge(3, 4)
    outer_joined = jnp.where(is_first, in_before, in_after)
    mate_joined = jnp.where(is_first, in_after, in_before)

    def finish(d, c, rows, carried):
        mix[d, :, part(c, chunk_cols)] = (local[d, c] + sc[1 - d, c] * dot(rows, carried)).astype(BF16)

    rows = (srw[other].astype(F32) * outer_joined).astype(BF16)

    def from_outside(c):
        arrived([outer_send(c)], has_outer)
        relay_send(c).start()
        finish(side, c, rows, zbuf[c])

    over(CHUNKS, from_outside)
    mate_rows = (srw[side].astype(F32) * joined).astype(BF16)
    arrived([gain_send])

    def from_mate(c):
        relay_send(c).wait_recv()
        carried = mbuf[c].astype(F32) + (gmate[c] * mate_joined) * lbuf[c].astype(F32)
        finish(other, c, mate_rows, carried.astype(BF16))


    left([docs_mate, kv_mate, q_mate, do_mate, gain_send])
    left(docs_after + kv_after, has_after)
    left(docs_before, has_before & is_first)

    def carries_left(c):
        mate_send(c).wait_send()
        left([outer_send(c)], has_outer)

    over(CHUNKS, carries_left)
    over(CHUNKS, from_mate)

    arrived([ao_mate, grads_mate])
    ao[other] = aom[...]
    arrived(grads_from, has_after)
    for n in range(2):
        gkv[side, n] = (gacc[own, n] + gr[side, n].astype(F32)).astype(BF16)
        gkv[other, n] = (grm[n].astype(F32) + gr[other, n].astype(F32)).astype(BF16)

    left([ao_mate, grads_mate])
    left([grads_before(0), grads_before(1)], has_before)
    over(CHUNKS, lambda c: relay_send(c).wait_send())


def store_kernel(ao, mix, gkv, ao_out, mo_out, gk_out, gv_out, gx_out, sem):
    moves = [(mix.at[0], mo_out), (mix.at[1], gx_out)]
    for h in range(2):
        wide = ao.shape[2]
        moves.append((ao.at[h], ao_out.at[:, pl.ds(h * wide, wide)]))
        for n, out in enumerate((gk_out, gv_out)):
            moves.append((gkv.at[h, n], out.at[:, pl.ds(h * HEAD_CHANNELS, HEAD_CHANNELS)]))
    copies = [pltpu.make_async_copy(src, dst, sem.at[n]) for n, (src, dst) in enumerate(moves)]
    for copy in copies:
        copy.start()
    for copy in copies:
        copy.wait()


def shards(q, k, v, x, ld, sw, sr, doc, do, cm):
    tokens = q.shape[0]
    assert k.shape[1] == 2 * HEAD_CHANNELS
    wide = q.shape[1] // 2
    heads = ld.shape[1]
    states = sw.shape[1]
    chunk_cols = x.shape[1] // CHUNKS
    span = 3 * tokens
    square = (tokens, HEAD_CHANNELS)
    vmem = pltpu.VMEM
    hbm = pl.BlockSpec(memory_space=pltpu.HBM)
    onchip = pl.BlockSpec(memory_space=pltpu.VMEM)
    shape = jax.ShapeDtypeStruct
    operands = [
        pltpu.with_memory_space_constraint(a, pltpu.HBM) for a in (q, k, v, x, ld.T, sw, sr, doc.reshape(1, tokens), do, cm)
    ]
    parts = pl.pallas_call(
        step_kernel,
        out_shape=(shape((2, tokens, wide), BF16), shape((2,) + x.shape, BF16), shape((2, 2) + square, BF16)),
        in_specs=[hbm] * 10,
        out_specs=[onchip] * 3,
        scratch_shapes=[
            vmem((2, tokens, wide), BF16),
            vmem((2, tokens, wide), BF16),
            vmem((2, CHUNKS, tokens, chunk_cols), BF16),
            vmem((heads, tokens), F32),
            vmem((2, tokens, states), BF16),
            vmem((2, states, tokens), F32),
            vmem((5, 1, tokens), jnp.int32),
            vmem((2, 2) + square, BF16),
            vmem((4, 2) + square, BF16),
            vmem((2, tokens, 2 * heads), BF16),
            vmem((2, CHUNKS, heads // CHUNKS, tokens), F32),
            vmem((2, CHUNKS, tokens, chunk_cols), F32),
            vmem((CHUNKS, heads // CHUNKS, tokens), F32),
            vmem((2, CHUNKS, states, chunk_cols), BF16),
            vmem((CHUNKS, states, chunk_cols), BF16),
            vmem((CHUNKS, states, chunk_cols), BF16),
            vmem((CHUNKS, states, chunk_cols), BF16),
            vmem((CHUNKS, states, chunk_cols), BF16),
            vmem((CHUNKS, 1, chunk_cols), F32),
            vmem((CHUNKS, 1, chunk_cols), F32),
            vmem((2, CHUNKS, tokens, chunk_cols), F32),
            vmem((wide // HEAD_CHANNELS // 2, span, 2 * tokens), BF16),
            vmem((wide // HEAD_CHANNELS // 2, span, 2 * tokens), BF16),
            vmem((span, tokens), F32),
            vmem((2, tokens, wide), BF16),
            vmem((tokens, wide), BF16),
            vmem((2, 2) + square, BF16),
            vmem((4, 2) + square, F32),
            vmem((2, 2) + square, BF16),
            vmem((2,) + square, BF16),
            vmem((2,) + square, BF16),
            vmem((2, tokens, tokens), F32),
            pltpu.SemaphoreType.DMA((14,)),
            pltpu.SemaphoreType.DMA((21 + 3 * CHUNKS,)),
            pltpu.SemaphoreType.DMA((14 + 3 * CHUNKS,)),
        ],
        compiler_params=pltpu.CompilerParams(collective_id=0, has_side_effects=True, vmem_limit_bytes=40 << 20),
        name="step",
    )(*operands)
    return pl.pallas_call(
        store_kernel,
        out_shape=(
            shape(q.shape, BF16), shape(x.shape, BF16), shape(k.shape, BF16), shape(v.shape, BF16), shape(x.shape, BF16),
        ),
        in_specs=[onchip] * 3,
        out_specs=[hbm] * 5,
        scratch_shapes=[pltpu.SemaphoreType.DMA((8,))],
        compiler_params=pltpu.CompilerParams(vmem_limit_bytes=8 << 20),
        name="store",
    )(*parts)


def solution(mesh):
    both = P("ctx", "tp")
    return jax.shard_map(
        shards,
        mesh=mesh,
        in_specs=(both, both, both, both, both, P("ctx", None), P("ctx", None), P("ctx"), both, both),
        out_specs=(both,) * 5,
        check_vma=False,
    )
```

time: 21.9 us -> 21.3 us (0.973)
  Pallas kernels: 21.1 us -> 20.5 us
    pallas_call x1, Pallas kernels: 19.9 us -> 19.4 us  [shards(): pl.pallas_call(step_kernel, out_shape=(shape((2, tokens, wide), BF16), sh...]
where the time goes in v3:
time: 21.3 us; the launch traced here: 21.2 us
  Pallas kernels  20.5 us (96%)
  between operations  0.64 us (3%)
    pallas_call x1, Pallas kernels, shards(): pl.pallas_call(step_kernel, out_shape=(shape((2, tokens, wide), BF16), sh...  19.4 us
    pallas_call x1, Pallas kernels, shards(): pl.pallas_call(store_kernel, out_shape=(shape(q.shape, BF16), shape(x.sha...  1.15 us

profile of v3, /device:TPU:23, one launch (start us, length us, event | category | flops | bytes accessed | tf_op | source)
XLA Modules:
  0.0 21.2 jit_solution(5841615880336138646)
XLA Ops:
  0.6 19.4 %step.1 = (bf16[2,128,512]{2,1,0:T(8,128)(2,1)S(1)}, bf16[2,128,2048]{2,1,0:T(8,128)(2,1)S(1)}, bf16[2,2,128,128]{3,2,1,0:T(8,128)(2,1)S(1)}) custom-call(bf16[128,1024]{1,0:T(8,128)(2,1)} %q_in.1, bf16[128,256]{1,0:T(8,128)(2,1)} %k_in.1, bf16[128,256]{1,0:T(8,128)(2,1)} %v_in.1, bf16[128,2048]{1,0:T(8,128)(2,1)} %x_in.1, f32[32,128]{1,0:T(8,128)} %bitcast.2, ...), custom_call_target="tpu_custom_call" | custom-call | tf_op jit(solution)/shard_map/step/pallas_call | solution.py:462
  20.0 1.2 %store.1 = (bf16[128,1024]{1,0:T(8,128)(2,1)}, bf16[128,2048]{1,0:T(8,128)(2,1)}, bf16[128,256]{1,0:T(8,128)(2,1)}, bf16[128,256]{1,0:T(8,128)(2,1)}, bf16[128,2048]{1,0:T(8,128)(2,1)}) custom-call(bf16[2,128,512]{2,1,0:T(8,128)(2,1)S(1)} %get-tuple-element.8.ao, bf16[2,128,2048]{2,1,0:T(8,128)(2,1)S(1)} %get-tuple-element.9.mix, ...), custom_call_target="tpu_custom_call" | custom-call | tf_op jit(solution)/shard_map/store/pallas_call | solution.py:507

commit v4 on v3

--- a/solution.py
+++ b/solution.py
@@ -9,6 +9,7 @@
 
 HEAD_CHANNELS = 128
 CHUNKS = 4
+DOUBLED = 128
 ROUND = 16
 MESH = pl.DeviceIdType.MESH
 F32 = jnp.float32
@@ -31,7 +32,7 @@
     q_in, k_in, v_in, x_in, ld_in, sw_in, sr_in, doc_in, do_in, cm_in,
     ao, mix, gkv,
     qw, dow, xc, ldb, srw, srwt, docs, kvo, kvw, scale, wrow, sc, lt, st, mbuf, cz, zbuf, lbuf, gain, gmate,
-    local, pt, dst, bias, aob, aom, gs, gacc, gr, gsm, grm, gmask, lsem, ssem, rsem,
+    local, pt, dst, bias, aob, aom, gs, gacc, gr, gsm, grm, gmask, lsem, ssem, rsem, ready,
 ):
     tokens = qw.shape[1]
     wide = qw.shape[2]
@@ -56,31 +57,34 @@
     has_before = me >= 2
     has_after = me < count - 2
     is_first = side == 0
+    at_front = has_before & (lax.rem(me, ROUND) < 2)
+    at_back = has_after & (lax.rem(me, ROUND) >= ROUND - 2)
     has_outer = (is_first & has_before) | (jnp.logical_not(is_first) & has_after)
 
-    local_at = [0]
-
-    def load(src, dst_ref):
-        copy = pltpu.make_async_copy(src, dst_ref, lsem.at[local_at[0]])
-        local_at[0] += 1
-        copy.start()
-        return copy
-
-    send_at = [0]
-    recv_at = [0]
-
-    def slot(at, n=1):
-        at[0] += n
-        return at[0] - n
-
-    def copy_to(src, dst_ref, target, recv):
+    sems = {}
+
+    def sem(kind, name, width=1):
+        ref, used = {"local": (lsem, 0), "send": (ssem, 1), "recv": (rsem, 2)}[kind]
+        if (kind, name) not in sems:
+            sems[kind, name] = sems.get(used, 0)
+            sems[used] = sems.get(used, 0) + width
+        return ref, sems[kind, name]
+
+    def drain(kind, name, ref, at=0):
+        array, first = sem(kind, name)
+        pltpu.make_async_copy(ref, ref, array.at[first + at]).wait()
+
+    def load(name, src, dst_ref):
+        array, first = sem("local", name)
+        pltpu.make_async_copy(src, dst_ref, array.at[first]).start()
+
+    def send(name, src, dst_ref, target, at=0, width=1):
+        out, out_first = sem("send", name)
+        into, into_first = sem("recv", name, width)
         return pltpu.make_async_remote_copy(
-            src_ref=src, dst_ref=dst_ref, send_sem=ssem.at[slot(send_at)], recv_sem=rsem.at[recv],
+            src_ref=src, dst_ref=dst_ref, send_sem=out.at[out_first], recv_sem=into.at[into_first + at],
             device_id=(target, row), device_id_type=MESH,
         )
-
-    def send(src, dst_ref, target):
-        return copy_to(src, dst_ref, target, slot(recv_at))
 
     def each(copies, act, there):
         if there is None:
@@ -95,11 +99,8 @@
     def start(copies, there=None):
         each(copies, lambda copy: copy.start(), there)
 
-    def arrived(copies, there=None):
-        each(copies, lambda copy: copy.wait_recv(), there)
-
-    def left(copies, there=None):
-        each(copies, lambda copy: copy.wait_send(), there)
+    def drained(kind, waits, there=None):
+        each(waits, lambda wait: drain(kind, *wait), there)
 
     def over(count, body):
         lax.fori_loop(0, count, lambda c, carry: (body(c), carry)[1], 0)
@@ -107,74 +108,67 @@
     def part(which, width):
         return pl.ds(pl.multiple_of(which * width, width), width)
 
-    docs_mate = send(docs.at[own], docs.at[own], mate)
-    at = slot(recv_at, 2)
-    docs_after = [copy_to(docs.at[own], docs.at[side], after[h], at + side) for h in range(2)]
-    docs_from = [copy_to(docs.at[own], docs.at[h], mate, at + h) for h in range(2)]
-    at = slot(recv_at)
-    docs_before = [copy_to(docs.at[2], docs.at[4], before[h], at) for h in range(2)]
-    kv_mate = send(kvo.at[other], kvw.at[own], mate)
-    at = slot(recv_at, 2)
-    kv_after = [copy_to(kvo.at[h], kvw.at[side], after[h], at + side) for h in range(2)]
-    kv_from = [copy_to(kvo.at[h], kvw.at[h], mate, at + h) for h in range(2)]
-    q_mate = send(q_in.at[:, part(other, wide)], qw.at[side], mate)
-    do_mate = send(do_in.at[:, part(other, wide)], dow.at[side], mate)
-    gain_send = send(gain, gmate, mate)
-
-    def chunked(src, dst_ref, target):
-        base_send, base_recv = slot(send_at, CHUNKS), slot(recv_at, CHUNKS)
-
-        def copy(c):
-            return pltpu.make_async_remote_copy(
-                src_ref=src.at[c], dst_ref=dst_ref.at[c], send_sem=ssem.at[base_send + c], recv_sem=rsem.at[base_recv + c],
-                device_id=(target, row), device_id_type=MESH,
-            )
-
-        return copy
-
-    mate_send = chunked(st.at[side], mbuf, mate)
-    outer_send = chunked(cz, zbuf, outer)
-    relay_send = chunked(zbuf, lbuf, mate)
-    ao_mate = send(aob.at[other], aom, mate)
-    at = slot(recv_at, 2)
-    grads_at = slot(send_at, 2)
+    docs_mate = send("docs_mate", docs.at[own], docs.at[own], mate)
+    docs_after = [send("docs_after", docs.at[own], docs.at[side], after[h]) for h in range(2)]
+    docs_before = [send("docs_before", docs.at[2], docs.at[4], before[h]) for h in range(2)]
+    kv_mate = send("kv_mate", kvo.at[other], kvw.at[own], mate)
+    kv_after = [send("kv_after", kvo.at[h], kvw.at[side], after[h]) for h in range(2)]
+    q_mate = send("q_mate", q_in.at[:, part(other, wide)], qw.at[side], mate)
+    do_mate = send("q_mate", do_in.at[:, part(other, wide)], dow.at[side], mate)
+    gain_send = send("gain", gain, gmate, mate)
+    ao_mate = send("ao", aob.at[other], aom, mate)
+    grads_mate = send("grads_mate", gsm, grm, mate)
+    sem("recv", "mate", CHUNKS)
+    sem("recv", "outer", CHUNKS)
+    sem("recv", "relay", CHUNKS)
 
     def grads_before(h):
-        return pltpu.make_async_remote_copy(
-            src_ref=gs.at[h], dst_ref=gr.at[side], send_sem=ssem.at[grads_at + h], recv_sem=rsem.at[at + side],
-            device_id=(before[0] + h, row), device_id_type=MESH,
-        )
-
-    grads_from = [copy_to(gs.at[h], gr.at[h], mate, at + h) for h in range(2)]
-    grads_mate = send(gsm, grm, mate)
+        return send("grads", gs.at[h], gr.at[side], before[0] + h)
+
+    def mate_send(c):
+        return send("mate", st.at[side, c], mbuf.at[c], mate, c)
+
+    def outer_send(c):
+        return send("outer", cz.at[c], zbuf.at[c], outer, c)
+
+    def relay_send(c):
+        return send("relay", zbuf.at[c], lbuf.at[c], mate, c)
+
+    last = CHUNKS - 1
+    halves = [pl.ds(0, chunk_cols - DOUBLED), pl.ds(chunk_cols - DOUBLED, DOUBLED)]
+    low_send = send("low", cz.at[last, :, halves[0]], zbuf.at[last, :, halves[0]], outer)
+    high_send = send("high", cz.at[last, :, halves[1]], zbuf.at[last, :, halves[1]], outer)
+    far_send = send("far", cz.at[last, :, halves[1]], lbuf.at[last, :, halves[1]], outer - 1 + 2 * side)
+    low_relay = send("low_relay", zbuf.at[last, :, halves[0]], lbuf.at[last, :, halves[0]], mate)
 
     barrier = pltpu.get_barrier_semaphore()
-    for there, targets in ((None, [mate]), (has_before, before), (has_after, after)):
+
+    def tell(semaphore, targets, there=None):
         each(
             targets,
-            lambda target: pl.semaphore_signal(barrier, inc=1, device_id=(target, row), device_id_type=MESH),
+            lambda target: pl.semaphore_signal(semaphore, inc=1, device_id=(target, row), device_id_type=MESH),
             there,
         )
 
-    doc_load = load(doc_in, docs.at[own])
-    kv_loads = []
+    tell(barrier, [mate])
+    tell(barrier, before, has_before)
+    tell(barrier, after, has_after & jnp.logical_not(at_back))
+
+    load("doc", doc_in, docs.at[own])
     for h in range(2):
         cols = pl.ds(h * HEAD_CHANNELS, HEAD_CHANNELS)
-        kv_loads += [load(k_in.at[:, cols], kvo.at[h, 0]), load(v_in.at[:, cols], kvo.at[h, 1])]
-    ld_load = load(ld_in, ldb)
-    sw_load = load(sw_in, srw.at[0])
-    sr_load = load(sr_in, srw.at[1])
-    x_at = local_at[0]
-    local_at[0] += 2
+        load("kv", k_in.at[:, cols], kvo.at[h, 0])
+        load("kv", v_in.at[:, cols], kvo.at[h, 1])
+    load("ld", ld_in, ldb)
+    load("states", sw_in, srw.at[0])
+    load("states", sr_in, srw.at[1])
     for d, src in enumerate((x_in, cm_in)):
         for c in range(CHUNKS):
-            pltpu.make_async_copy(src.at[:, pl.ds(c * chunk_cols, chunk_cols)], xc.at[d, c], lsem.at[x_at + d]).start()
-    own_loads = [
-        load(k_in.at[:, part(side, HEAD_CHANNELS)], kvw.at[own, 0]),
-        load(v_in.at[:, part(side, HEAD_CHANNELS)], kvw.at[own, 1]),
-        load(q_in.at[:, part(side, wide)], qw.at[side]),
-        load(do_in.at[:, part(side, wide)], dow.at[side]),
-    ]
+            load("x", src.at[:, pl.ds(c * chunk_cols, chunk_cols)], xc.at[d, c])
+    load("own_kv", k_in.at[:, part(side, HEAD_CHANNELS)], kvw.at[own, 0])
+    load("own_kv", v_in.at[:, part(side, HEAD_CHANNELS)], kvw.at[own, 1])
+    load("q", q_in.at[:, part(side, wide)], qw.at[side])
+    load("q", do_in.at[:, part(side, wide)], dow.at[side])
 
     @pl.when(jnp.logical_not(has_before))
     def _():
@@ -191,17 +185,21 @@
     def _():
         zbuf[...] = jnp.zeros(zbuf.shape, BF16)
 
+    @pl.when(jnp.logical_not(is_first | has_before))
+    def _():
+        lbuf[last] = jnp.zeros(lbuf.shape[1:], BF16)
+
     def announce():
-        pl.semaphore_wait(barrier, 1 + 2 * has_before.astype(jnp.int32) + 2 * has_after.astype(jnp.int32))
+        greeted = (has_before & jnp.logical_not(at_front)).astype(jnp.int32) + has_after.astype(jnp.int32)
+        pl.semaphore_wait(barrier, 1 + 2 * greeted)
+        tell(ready, after, at_back)
         start([docs_mate])
         start(docs_after + kv_after, has_after)
-        start(docs_before, has_before & is_first)
+        start(docs_before, has_before & is_first & jnp.logical_not(at_front))
         start([kv_mate, q_mate, do_mate])
 
     sends_early = lax.rem(me, ROUND) >= ROUND // 2
-    doc_load.wait()
-    for copy in kv_loads:
-        copy.wait()
+    drained("local", [("doc", docs.at[own]), ("kv", kvo)])
 
     @pl.when(sends_early)
     def _():
@@ -210,7 +208,7 @@
     rows_i = lax.broadcasted_iota(jnp.int32, square, 0)
     cols_i = lax.broadcasted_iota(jnp.int32, square, 1)
     triu = (rows_i <= cols_i).astype(F32).astype(BF16)
-    ld_load.wait()
+    drained("local", [("ld", ldb)])
     sums = dot(bf16_parts(ldb[...], 3), triu)
     lam_t = (sums[2 * heads :] + sums[heads : 2 * heads]) + sums[:heads]
     for c in range(CHUNKS):
@@ -226,8 +224,7 @@
     doc_last = doc_row[:, tokens - 1 : tokens]
     doc_rows = jnp.broadcast_to(doc_row, square)
     doc_cols = doc_rows.T
-    sw_load.wait()
-    sr_load.wait()
+    drained("local", [("states", srw)])
     writes = srw[0]
     reads = srw[1]
     writes_in = jnp.where(doc_cols == doc_last, writes.astype(F32), 0.0)
@@ -251,8 +248,7 @@
             left_side = [(srwt[d] * weights[h : h + 1]).astype(BF16) for h in (2 * j, 2 * j + 1)]
             st[d, c, :, cols] = dot(jnp.concatenate(left_side, axis=1), two_heads(xc[d, c, :, cols])).astype(BF16)
 
-    for d in range(2):
-        pltpu.make_async_copy(xc.at[d], xc.at[d], lsem.at[x_at + d]).wait()
+    drained("local", [("x", xc)])
 
     def first_state(c):
         state(side, c)
@@ -283,15 +279,21 @@
         ends = docs[early].astype(F32)[:, tokens - 1 : tokens]
         return (docs[late].astype(F32)[:, 0:1] == ends).astype(F32)
 
-    arrived([docs_mate])
+    drained("recv", [("docs_mate", docs.at[own])])
     joined = edge(2, 3)
 
     def combine(c):
-        mate_send(c).wait_recv()
+        drain("recv", "mate", mbuf.at[c], c)
         cz[c] = (st[other, c].astype(F32) + (gain[c] * joined) * mbuf[c].astype(F32)).astype(BF16)
-        start([outer_send(c)], has_outer)
+        start([outer_send(c)], has_outer & (is_first | (c < last)))
+
+    @pl.when(at_front & is_first)
+    def _():
+        pl.semaphore_wait(ready, 2)
+        start(docs_before)
 
     over(CHUNKS, combine)
+    start([low_send, far_send, high_send], has_outer & jnp.logical_not(is_first))
 
     scale[0] = bf16_parts(exits, 2).T
     scale[1] = bf16_parts(entries, 2).T
@@ -321,11 +323,13 @@
 
     over(CHUNKS, inside_block)
 
-    arrived(docs_from, has_before)
-    for copy in own_loads:
-        copy.wait()
-    arrived([q_mate, do_mate, kv_mate])
-    arrived(kv_from, has_before)
+    @pl.when(at_front & jnp.logical_not(is_first))
+    def _():
+        pl.semaphore_wait(ready, 2)
+
+    drained("local", [("own_kv", kvw.at[own]), ("q", qw)])
+    drained("recv", [("q_mate", qw), ("kv_mate", kvw.at[own])])
+    drained("recv", [("docs_after", docs.at[0:2]), ("kv_after", kvw.at[0:2])], has_before)
     gacc[...] = jnp.zeros(gacc.shape, F32)
 
     def attend(pos):
@@ -380,7 +384,7 @@
     start([grads_mate])
     ao[side] = aob[side]
 
-    arrived([docs_before[0]], has_after)
+    drained("recv", [("docs_before", docs.at[4])], has_after)
     in_before = edge(1, 2)
     in_after = edge(3, 4)
     outer_joined = jnp.where(is_first, in_before, in_after)
@@ -392,41 +396,70 @@
     rows = (srw[other].astype(F32) * outer_joined).astype(BF16)
 
     def from_outside(c):
-        arrived([outer_send(c)], has_outer)
+        drained("recv", [("outer", zbuf.at[c], c)], has_outer)
         relay_send(c).start()
         finish(side, c, rows, zbuf[c])
 
-    over(CHUNKS, from_outside)
+    over(last, from_outside)
+
+    @pl.when(is_first)
+    def _():
+        drained("recv", [("low", zbuf.at[last, :, halves[0]])], has_outer)
+        low_relay.start()
+        drained("recv", [("high", zbuf.at[last, :, halves[1]])], has_outer)
+
+    @pl.when(jnp.logical_not(is_first))
+    def _():
+        drained("recv", [("outer", zbuf.at[last], last)], has_outer)
+        relay_send(last).start()
+
+    finish(side, last, rows, zbuf[last])
     mate_rows = (srw[side].astype(F32) * joined).astype(BF16)
-    arrived([gain_send])
-
-    def from_mate(c):
-        relay_send(c).wait_recv()
+    drained("recv", [("gain", gain)])
+
+    def carry_from_mate(c):
         carried = mbuf[c].astype(F32) + (gmate[c] * mate_joined) * lbuf[c].astype(F32)
         finish(other, c, mate_rows, carried.astype(BF16))
 
-
-    left([docs_mate, kv_mate, q_mate, do_mate, gain_send])
-    left(docs_after + kv_after, has_after)
-    left(docs_before, has_before & is_first)
-
-    def carries_left(c):
-        mate_send(c).wait_send()
-        left([outer_send(c)], has_outer)
-
-    over(CHUNKS, carries_left)
-    over(CHUNKS, from_mate)
-
-    arrived([ao_mate, grads_mate])
+    def from_mate(c):
+        drain("recv", "relay", lbuf.at[c], c)
+        carry_from_mate(c)
+
+    sent = [("docs_mate", docs.at[own]), ("kv_mate", kvo.at[0]), ("q_mate", qw), ("gain", gain), ("mate", mbuf)]
+    drained("send", sent)
+    drained("send", [("docs_after", docs.at[0:2]), ("kv_after", kvo)], has_after)
+    drained("send", [("docs_before", docs.at[0:2])], has_before & is_first)
+    drained("send", [("outer", cz)], has_outer & is_first)
+    low_part, high_part = (cz.at[last, :, cols] for cols in halves)
+    drained(
+        "send",
+        [("outer", cz.at[0:last]), ("low", low_part), ("high", high_part), ("far", high_part)],
+        has_outer & jnp.logical_not(is_first),
+    )
+    over(last, from_mate)
+
+    @pl.when(is_first)
+    def _():
+        drained("recv", [("relay", lbuf.at[last], last)])
+
+    @pl.when(jnp.logical_not(is_first))
+    def _():
+        drained("recv", [("low_relay", lbuf.at[last, :, halves[0]])])
+        drained("recv", [("far", lbuf.at[last, :, halves[1]])], has_before)
+
+    carry_from_mate(last)
+
+    drained("recv", [("ao", aom), ("grads_mate", grm)])
     ao[other] = aom[...]
-    arrived(grads_from, has_after)
+    drained("recv", [("grads", gr)], has_after)
     for n in range(2):
         gkv[side, n] = (gacc[own, n] + gr[side, n].astype(F32)).astype(BF16)
         gkv[other, n] = (grm[n].astype(F32) + gr[other, n].astype(F32)).astype(BF16)
 
-    left([ao_mate, grads_mate])
-    left([grads_before(0), grads_before(1)], has_before)
-    over(CHUNKS, lambda c: relay_send(c).wait_send())
+    drained("send", [("ao", aom), ("grads_mate", gsm)])
+    drained("send", [("grads", gs)], has_before)
+    drained("send", [("relay", zbuf.at[0:last]), ("low_relay", low_part)], is_first)
+    drained("send", [("relay", zbuf)], jnp.logical_not(is_first))
 
 
 def store_kernel(ao, mix, gkv, ao_out, mo_out, gk_out, gv_out, gx_out, sem):
@@ -497,9 +530,10 @@
             vmem((2,) + square, BF16),
             vmem((2,) + square, BF16),
             vmem((2, tokens, tokens), F32),
-            pltpu.SemaphoreType.DMA((14,)),
-            pltpu.SemaphoreType.DMA((21 + 3 * CHUNKS,)),
+            pltpu.SemaphoreType.DMA((7,)),
+            pltpu.SemaphoreType.DMA((17,)),
             pltpu.SemaphoreType.DMA((14 + 3 * CHUNKS,)),
+            pltpu.SemaphoreType.REGULAR,
         ],
         compiler_params=pltpu.CompilerParams(collective_id=0, has_side_effects=True, vmem_limit_bytes=40 << 20),
         name="step",

time: 21.3 us -> 20.9 us (0.981)
  Pallas kernels: 20.5 us -> 19.9 us
    pallas_call x1, Pallas kernels: 19.4 us -> 18.8 us  [shards(): pl.pallas_call(step_kernel, out_shape=(shape((2, tokens, wide), BF16), sh...]
where the time goes in v4:
time: 20.9 us; the launch traced here: 20.6 us
  Pallas kernels  19.9 us (95%)
  between operations  0.64 us (3%)
    pallas_call x1, Pallas kernels, shards(): pl.pallas_call(step_kernel, out_shape=(shape((2, tokens, wide), BF16), sh...  18.8 us
    pallas_call x1, Pallas kernels, shards(): pl.pallas_call(store_kernel, out_shape=(shape(q.shape, BF16), shape(x.sha...  1.15 us

profile of v4, /device:TPU:23, one launch (start us, length us, event | category | flops | bytes accessed | tf_op | source)
XLA Modules:
  0.0 20.6 jit_solution(6389272311651852320)
XLA Ops:
  0.6 18.8 %step.1 = (bf16[2,128,512]{2,1,0:T(8,128)(2,1)S(1)}, bf16[2,128,2048]{2,1,0:T(8,128)(2,1)S(1)}, bf16[2,2,128,128]{3,2,1,0:T(8,128)(2,1)S(1)}) custom-call(bf16[128,1024]{1,0:T(8,128)(2,1)} %q_in.1, bf16[128,256]{1,0:T(8,128)(2,1)} %k_in.1, bf16[128,256]{1,0:T(8,128)(2,1)} %v_in.1, bf16[128,2048]{1,0:T(8,128)(2,1)} %x_in.1, f32[32,128]{1,0:T(8,128)} %bitcast.2, ...), custom_call_target="tpu_custom_call" | custom-call | tf_op jit(solution)/shard_map/step/pallas_call | solution.py:495
  19.4 1.2 %store.1 = (bf16[128,1024]{1,0:T(8,128)(2,1)}, bf16[128,2048]{1,0:T(8,128)(2,1)}, bf16[128,256]{1,0:T(8,128)(2,1)}, bf16[128,256]{1,0:T(8,128)(2,1)}, bf16[128,2048]{1,0:T(8,128)(2,1)}) custom-call(bf16[2,128,512]{2,1,0:T(8,128)(2,1)S(1)} %get-tuple-element.8.ao, bf16[2,128,2048]{2,1,0:T(8,128)(2,1)S(1)} %get-tuple-element.9.mix, ...), custom_call_target="tpu_custom_call" | custom-call | tf_op jit(solution)/shard_map/store/pallas_call | solution.py:541

commit v5 on v4

--- a/solution.py
+++ b/solution.py
@@ -9,7 +9,7 @@
 
 HEAD_CHANNELS = 128
 CHUNKS = 4
-DOUBLED = 128
+DOUBLED = 256
 ROUND = 16
 MESH = pl.DeviceIdType.MESH
 F32 = jnp.float32
@@ -395,6 +395,39 @@
 
     rows = (srw[other].astype(F32) * outer_joined).astype(BF16)
 
+    mate_rows = (srw[side].astype(F32) * joined).astype(BF16)
+
+    def carry_from_mate(c):
+        carried = mbuf[c].astype(F32) + (gmate[c] * mate_joined) * lbuf[c].astype(F32)
+        finish(other, c, mate_rows, carried.astype(BF16))
+
+    def from_mate(c):
+        drain("recv", "relay", lbuf.at[c], c)
+        carry_from_mate(c)
+
+    def carries_from_mate():
+        drained("recv", [("gain", gain)])
+        over(last, from_mate)
+
+        @pl.when(is_first)
+        def _():
+            drained("recv", [("relay", lbuf.at[last], last)])
+
+        @pl.when(jnp.logical_not(is_first))
+        def _():
+            drained("recv", [("low_relay", lbuf.at[last, :, halves[0]])])
+            drained("recv", [("far", lbuf.at[last, :, halves[1]])], has_before)
+
+        carry_from_mate(last)
+
+    def gradients():
+        drained("recv", [("ao", aom), ("grads_mate", grm)])
+        ao[other] = aom[...]
+        drained("recv", [("grads", gr)], has_after)
+        for n in range(2):
+            gkv[side, n] = (gacc[own, n] + gr[side, n].astype(F32)).astype(BF16)
+            gkv[other, n] = (grm[n].astype(F32) + gr[other, n].astype(F32)).astype(BF16)
+
     def from_outside(c):
         drained("recv", [("outer", zbuf.at[c], c)], has_outer)
         relay_send(c).start()
@@ -406,6 +439,11 @@
     def _():
         drained("recv", [("low", zbuf.at[last, :, halves[0]])], has_outer)
         low_relay.start()
+
+        @pl.when(at_front)
+        def _():
+            carries_from_mate()
+
         drained("recv", [("high", zbuf.at[last, :, halves[1]])], has_outer)
 
     @pl.when(jnp.logical_not(is_first))
@@ -414,17 +452,6 @@
         relay_send(last).start()
 
     finish(side, last, rows, zbuf[last])
-    mate_rows = (srw[side].astype(F32) * joined).astype(BF16)
-    drained("recv", [("gain", gain)])
-
-    def carry_from_mate(c):
-        carried = mbuf[c].astype(F32) + (gmate[c] * mate_joined) * lbuf[c].astype(F32)
-        finish(other, c, mate_rows, carried.astype(BF16))
-
-    def from_mate(c):
-        drain("recv", "relay", lbuf.at[c], c)
-        carry_from_mate(c)
-
     sent = [("docs_mate", docs.at[own]), ("kv_mate", kvo.at[0]), ("q_mate", qw), ("gain", gain), ("mate", mbuf)]
     drained("send", sent)
     drained("send", [("docs_after", docs.at[0:2]), ("kv_after", kvo)], has_after)
@@ -436,26 +463,12 @@
         [("outer", cz.at[0:last]), ("low", low_part), ("high", high_part), ("far", high_part)],
         has_outer & jnp.logical_not(is_first),
     )
-    over(last, from_mate)
-
-    @pl.when(is_first)
-    def _():
-        drained("recv", [("relay", lbuf.at[last], last)])
-
-    @pl.when(jnp.logical_not(is_first))
-    def _():
-        drained("recv", [("low_relay", lbuf.at[last, :, halves[0]])])
-        drained("recv", [("far", lbuf.at[last, :, halves[1]])], has_before)
-
-    carry_from_mate(last)
-
-    drained("recv", [("ao", aom), ("grads_mate", grm)])
-    ao[other] = aom[...]
-    drained("recv", [("grads", gr)], has_after)
-    for n in range(2):
-        gkv[side, n] = (gacc[own, n] + gr[side, n].astype(F32)).astype(BF16)
-        gkv[other, n] = (grm[n].astype(F32) + gr[other, n].astype(F32)).astype(BF16)
-
+
+    @pl.when(jnp.logical_not(at_front & is_first))
+    def _():
+        carries_from_mate()
+
+    gradients()
     drained("send", [("ao", aom), ("grads_mate", gsm)])
     drained("send", [("grads", gs)], has_before)
     drained("send", [("relay", zbuf.at[0:last]), ("low_relay", low_part)], is_first)

time: 20.9 us -> 20.3 us (0.971)
  Pallas kernels: 19.9 us -> 19.5 us
    pallas_call x1, Pallas kernels: 18.8 us -> 18.4 us  [shards(): pl.pallas_call(step_kernel, out_shape=(shape((2, tokens, wide), BF16), sh...]
where the time goes in v5:
time: 20.3 us; the launch traced here: 20.2 us
  Pallas kernels  19.5 us (96%)
  between operations  0.64 us (3%)
    pallas_call x1, Pallas kernels, shards(): pl.pallas_call(step_kernel, out_shape=(shape((2, tokens, wide), BF16), sh...  18.4 us
    pallas_call x1, Pallas kernels, shards(): pl.pallas_call(store_kernel, out_shape=(shape(q.shape, BF16), shape(x.sha...  1.15 us

profile of v5, /device:TPU:23, one launch (start us, length us, event | category | flops | bytes accessed | tf_op | source)
XLA Modules:
  0.0 20.2 jit_solution(3403637572394862707)
XLA Ops:
  0.6 18.4 %step.1 = (bf16[2,128,512]{2,1,0:T(8,128)(2,1)S(1)}, bf16[2,128,2048]{2,1,0:T(8,128)(2,1)S(1)}, bf16[2,2,128,128]{3,2,1,0:T(8,128)(2,1)S(1)}) custom-call(bf16[128,1024]{1,0:T(8,128)(2,1)} %q_in.1, bf16[128,256]{1,0:T(8,128)(2,1)} %k_in.1, bf16[128,256]{1,0:T(8,128)(2,1)} %v_in.1, bf16[128,2048]{1,0:T(8,128)(2,1)} %x_in.1, f32[32,128]{1,0:T(8,128)} %bitcast.2, ...), custom_call_target="tpu_custom_call" | custom-call | tf_op jit(solution)/shard_map/step/pallas_call | solution.py:508
  19.0 1.2 %store.1 = (bf16[128,1024]{1,0:T(8,128)(2,1)}, bf16[128,2048]{1,0:T(8,128)(2,1)}, bf16[128,256]{1,0:T(8,128)(2,1)}, bf16[128,256]{1,0:T(8,128)(2,1)}, bf16[128,2048]{1,0:T(8,128)(2,1)}) custom-call(bf16[2,128,512]{2,1,0:T(8,128)(2,1)S(1)} %get-tuple-element.8.ao, bf16[2,128,2048]{2,1,0:T(8,128)(2,1)S(1)} %get-tuple-element.9.mix, ...), custom_call_target="tpu_custom_call" | custom-call | tf_op jit(solution)/shard_map/store/pallas_call | solution.py:554

commit v6 on v5

--- a/solution.py
+++ b/solution.py
@@ -409,6 +409,10 @@
         drained("recv", [("gain", gain)])
         over(last, from_mate)
 
+        @pl.when(at_front & jnp.logical_not(is_first))
+        def _():
+            gradients()
+
         @pl.when(is_first)
         def _():
             drained("recv", [("relay", lbuf.at[last], last)])
@@ -443,6 +447,7 @@
         @pl.when(at_front)
         def _():
             carries_from_mate()
+            gradients()
 
         drained("recv", [("high", zbuf.at[last, :, halves[1]])], has_outer)
 
@@ -468,7 +473,10 @@
     def _():
         carries_from_mate()
 
-    gradients()
+    @pl.when(jnp.logical_not(at_front))
+    def _():
+        gradients()
+
     drained("send", [("ao", aom), ("grads_mate", gsm)])
     drained("send", [("grads", gs)], has_before)
     drained("send", [("relay", zbuf.at[0:last]), ("low_relay", low_part)], is_first)

time: 20.3 us -> 20.2 us (level)
  no operation moved by 1% of the time
where the time goes in v6:
time: 20.2 us; the launch traced here: 20.1 us
  Pallas kernels  19.5 us (97%)
  between operations  0.64 us (3%)
    pallas_call x1, Pallas kernels, shards(): pl.pallas_call(step_kernel, out_shape=(shape((2, tokens, wide), BF16), sh...  18.3 us
    pallas_call x1, Pallas kernels, shards(): pl.pallas_call(store_kernel, out_shape=(shape(q.shape, BF16), shape(x.sha...  1.15 us

profile of v6, /device:TPU:23, one launch (start us, length us, event | category | flops | bytes accessed | tf_op | source)
XLA Modules:
  0.0 20.1 jit_solution(13505372467719244016)
XLA Ops:
  0.6 18.3 %step.1 = (bf16[2,128,512]{2,1,0:T(8,128)(2,1)S(1)}, bf16[2,128,2048]{2,1,0:T(8,128)(2,1)S(1)}, bf16[2,2,128,128]{3,2,1,0:T(8,128)(2,1)S(1)}) custom-call(bf16[128,1024]{1,0:T(8,128)(2,1)} %q_in.1, bf16[128,256]{1,0:T(8,128)(2,1)} %k_in.1, bf16[128,256]{1,0:T(8,128)(2,1)} %v_in.1, bf16[128,2048]{1,0:T(8,128)(2,1)} %x_in.1, f32[32,128]{1,0:T(8,128)} %bitcast.2, ...), custom_call_target="tpu_custom_call" | custom-call | tf_op jit(solution)/shard_map/step/pallas_call | solution.py:516
  19.0 1.2 %store.1 = (bf16[128,1024]{1,0:T(8,128)(2,1)}, bf16[128,2048]{1,0:T(8,128)(2,1)}, bf16[128,256]{1,0:T(8,128)(2,1)}, bf16[128,256]{1,0:T(8,128)(2,1)}, bf16[128,2048]{1,0:T(8,128)(2,1)}) custom-call(bf16[2,128,512]{2,1,0:T(8,128)(2,1)S(1)} %get-tuple-element.8.ao, bf16[2,128,2048]{2,1,0:T(8,128)(2,1)S(1)} %get-tuple-element.9.mix, ...), custom_call_target="tpu_custom_call" | custom-call | tf_op jit(solution)/shard_map/store/pallas_call | solution.py:562
